TPU v7x, 256 devices: a whole 4x4x8 slice. The times are simulated.
256 devices in a mesh: section: 2 (over core), ctx: 32 (over z, x), mp: 4 (over y).
Axes of the slice: x: 4, y: 4, z: 8, core: 2. Of those that a mesh axis runs over, the one named last changes fastest.
Arguments:
- hidden: bfloat16 [2, 4096, 4672], P('section', 'ctx', 'mp'), may hold values from -120 to 120
- query: bfloat16 [2, 4096, 2048], P('section', 'ctx', 'mp'), may hold values from -6 to 6
- keys: bfloat16 [2, 4096, 2048], P('section', 'ctx', 'mp'), may hold values from -100 to 100
- values: bfloat16 [2, 4096, 2048], P('section', 'ctx', 'mp'), may hold values from -12 to 12
- w_out: bfloat16 [2, 4672, 2048], P('section', 'ctx', 'mp'), may hold values from -0.125 to 0.125
Outputs:
- handed: bfloat16 [2, 4096, 4672], P('section', 'ctx', 'mp')
- context: bfloat16 [2, 4096, 2048], P('section', 'ctx', 'mp')
All inputs are finite; a program needn't handle non-finite values.
Results may differ from a plain program's by a relative error of at most 0.0075.
Values may be sent and summed in bfloat16 or wider, within the bound.
No kernel may reach another device: no remote copies, remote signals or barrier semaphores. Data moves between devices by JAX's collectives and lax.ppermute only.
A program may use at most 128 MiB of HBM per device.

v0:
```python
import jax
import jax.numpy as jnp
from jax import lax
from jax.sharding import PartitionSpec as P

HEAD_DIM = 64


def from_behind(block, axis, distance):
    devices = range(lax.axis_size(axis))
    route = [((i - distance) % len(devices), i) for i in devices]
    return lax.ppermute(block, axis, route)


def head_scores(query_h, keys_h):
    return jnp.einsum("qd,kd->qk", query_h, keys_h, preferred_element_type=jnp.float32)


def body(hidden, query, keys, values, w_out):
    rows = hidden[0]
    query_rows = query[0]
    inner_dev = query_rows.shape[1]
    heads_dev = inner_dev // HEAD_DIM
    keys_local = keys[0]
    values_local = values[0]
    keys_all, values_all = (
        lax.all_gather(keys_local, "ctx", axis=0, tiled=True),
        lax.all_gather(values_local, "ctx", axis=0, tiled=True),
    )
    pieces = []
    for head in range(heads_dev):
        lower = head * HEAD_DIM
        upper = lower + HEAD_DIM
        scores = head_scores(query_rows[:, lower:upper], keys_all[:, lower:upper])
        peak = jnp.max(scores, axis=1, keepdims=True)
        expo = jnp.exp(scores - peak)
        total = jnp.sum(expo, axis=1, keepdims=True)
        summed = jnp.dot(
            expo.astype(jnp.bfloat16),
            values_all[:, lower:upper],
            preferred_element_type=jnp.float32,
        )
        pieces.append(summed / total)
    context = jnp.concatenate(pieces, axis=1).astype(jnp.bfloat16)
    out_local = w_out[0]
    branch_terms = jnp.einsum(
        "ri,di->rd",
        context,
        lax.all_gather(out_local, "ctx", axis=0, tiled=True),
        preferred_element_type=jnp.float32,
    )
    branch = lax.psum_scatter(
        branch_terms.astype(jnp.bfloat16), "mp", scatter_dimension=1, tiled=True
    ).astype(jnp.float32)
    result = (rows.astype(jnp.float32) + branch).astype(jnp.bfloat16)
    handed = from_behind(result, "section", 1)
    return (handed[None], context[None])


def solution(mesh):
    in_specs = (
        P("section", "ctx", "mp"),
        P("section", "ctx", "mp"),
        P("section", "ctx", "mp"),
        P("section", "ctx", "mp"),
        P("section", "ctx", "mp"),
    )
    out_specs = (P("section", "ctx", "mp"), P("section", "ctx", "mp"))
    return jax.shard_map(body, mesh=mesh, in_specs=in_specs, out_specs=out_specs, check_vma=False)
```

profile of v0, /device:TPU:1, one launch (start us, length us, event | category | flops | bytes accessed | tf_op | source)
XLA Modules:
  0.0 321.6 jit_solution(12413351099440571113)
XLA Ops:
  8.7 1.9 copy.10
  10.6 82.0 %all-gather.7.cloned.1.call-done = bf16[1,4096,512]{2,1,0:T(8,128)(2,1)} async-done(((bf16[1,128,512]{2,1,0:T(8,128)(2,1)}), bf16[1,4096,512]{2,1,0:T(8,128)(2,1)}) %all-gather.7.cloned.1.call-update) | async-done | bytes 4194320 | tf_op jit(solution)/shard_map/all_gather | solution.py:27
  92.6 1.8 fusion.75
  96.1 1.9 fusion.76
  99.8 1.8 fusion.77
  103.3 1.9 fusion.78
  107.0 1.8 fusion.79
  110.6 1.9 fusion.80
  112.5 1.4 copy-done.2
  114.3 1.8 fusion.81
  116.5 2.2 fusion.82
  119.2 54.6 %all-gather.9.cloned.1.call-done = bf16[1,4096,512]{2,1,0:T(8,128)(2,1)} async-done(((bf16[1,128,512]{2,1,0:T(8,128)(2,1)}), bf16[1,4096,512]{2,1,0:T(8,128)(2,1)}) %all-gather.9.cloned.1.call-update) | async-done | bytes 4194320 | tf_op jit(solution)/shard_map/all_gather | solution.py:28
  173.7 2.6 constant_dynamic-update-slice_fusion.7
  176.4 2.4 constant_dynamic-update-slice_fusion.6
  178.8 2.0 constant_dynamic-update-slice_fusion.5
  180.9 2.4 constant_dynamic-update-slice_fusion.4
  183.3 2.0 constant_dynamic-update-slice_fusion.3
  185.4 2.4 constant_dynamic-update-slice_fusion.2
  187.8 1.9 constant_dynamic-update-slice_fusion.1
  189.7 2.5 constant_dynamic-update-slice_fusion
  192.2 88.1 %all-gather.11.cloned.1.call-done = bf16[1,4672,512]{2,0,1:T(2,128)(2,1)} async-done(((bf16[1,146,512]{2,0,1:T(2,128)(2,1)}), bf16[1,4672,512]{2,0,1:T(2,128)(2,1)}) %all-gather.11.cloned.1.call-update) | async-done | bytes 4784144 | tf_op jit(solution)/shard_map/all_gather | solution.py:49
  280.3 6.2 %convolution_convert_fusion = bf16[128,4672]{0,1:T(8,128)(2,1)} fusion(bf16[128,512]{0,1:T(8,128)(2,1)S(1)} %get-tuple-element.38, bf16[1,4672,512]{2,0,1:T(2,128)(2,1)} %all-gather.11.cloned.1.call-done), kind=kOutput, calls=%fused_computation | convolution fusion | flops 612966400 | bytes 6111232 | tf_op jit(solution)/shard_map/ri,di->rd/dot_general | solution.py:46
  286.6 23.2 %reduce-scatter.2.cloned.1.call-done = bf16[128,1168]{0,1:T(8,128)(2,1)} async-done(((bf16[128,4672]{0,1:T(8,128)(2,1)}), bf16[128,1168]{0,1:T(8,128)(2,1)}) %reduce-scatter.2.cloned.1.call-update) | async-done | bytes 299024 | tf_op jit(solution)/shard_map/reduce_scatter | solution.py:52
  310.8 2.3 collective-permute-start
  (55 shorter events, 14.8 us)
Async XLA Ops:
  7.2 85.4 %all-gather.7.cloned.1.call-start = ((), (), s32[]{:S(2)}) async-start(), calls=%async_computation.2 | async-start | bytes 4325376 | tf_op jit(solution)/shard_map/all_gather | solution.py:27
  7.9 165.8 %all-gather.9.cloned.1.call-start = ((), (), s32[]{:S(2)}) async-start(), calls=%async_computation.3 | async-start | bytes 4325376 | tf_op jit(solution)/shard_map/all_gather | solution.py:28
  8.6 271.6 %all-gather.11.cloned.1.call-start = ((), (), s32[]{:S(2)}) async-start(), calls=%async_computation.4 | async-start | bytes 9867264 | tf_op jit(solution)/shard_map/all_gather | solution.py:49
  10.6 299.2 %reduce-scatter.2.cloned.1.call-start = ((), (), s32[]{:S(2)}) async-start(), calls=%async_computation.1 | async-start | bytes 1495040 | tf_op jit(solution)/shard_map/reduce_scatter | solution.py:52
  94.4 1.3 copy-start.12
  98.0 1.4 copy-start.10
  101.6 1.4 copy-start.8
  105.2 1.4 copy-start.6
  108.8 1.3 copy-start.4
  112.5 1.4 copy-start.2
  116.1 2.6 copy-start
  173.7 2.6 copy-start.11
  176.4 2.5 copy-start.9
  178.8 2.0 copy-start.7
  180.8 2.5 copy-start.5
  183.3 2.0 copy-start.3
  185.3 2.5 copy-start.1
  280.3 29.5 %copy-start.13 = (bf16[1,128,1168]{1,2,0:T(8,128)(2,1)S(1)}, bf16[1,128,1168]{1,2,0:T(8,128)(2,1)}, u32[]{:S(2)}) copy-start(bf16[1,128,1168]{1,2,0:T(8,128)(2,1)} %param.5) | copy-start | bytes 897028
  310.8 3.6 %collective-permute-start = (bf16[128,1168]{0,1:T(8,128)(2,1)S(1)}, bf16[128,1168]{0,1:T(8,128)(2,1)S(1)}, u32[]{:S(2)}, u32[]{:S(2)}) collective-permute-start(bf16[128,1168]{0,1:T(8,128)(2,1)S(1)} %fusion.66), channel_id=1, source_target_pairs={{128,0},{0,128},{129,1},{1,129},{130,2},{2,130},{131,3},{3,131},{1... | collective-permute-start | bytes 897032 | tf_op jit(solution)/shard_map/ppermute | solution.py:12
Sparse Core Ops, SparseCore 0:
  10.6 81.9 all-gather.6
  95.2 78.5 all-gather.8
  176.9 103.3 all-gather.10
  286.6 23.1 reduce-scatter.1
where the time goes:
time: 322 us
  waiting for transfers between devices  250 us (78%)
  matrix products  39.4 us (12%)
  between operations  14 us (4%)
  local copies, waits for them, and re-layouts  11.6 us (4%)
  other arithmetic  4.54 us (1%)
    all_gather x1, waiting for transfers between devices, body(): lax.all_gather(out_local, 'ctx', axis=0, tiled=True)  88.1 us
    all_gather x1, waiting for transfers between devices, body(): lax.all_gather(keys_local, 'ctx', axis=0, tiled=True)  82 us
    all_gather x1, waiting for transfers between devices, body(): lax.all_gather(values_local, 'ctx', axis=0, tiled=True)  54.6 us
    reduce_scatter x1, waiting for transfers between devices, body(): lax.psum_scatter(branch_terms.astype(jnp.bfloat16), 'mp', scatter_dimensi...  23.2 us
    dot_general x8, matrix products, body(): jnp.dot(expo.astype(jnp.bfloat16), values_all[:, lower:upper], preferred_...  18.3 us
    dot_general x8, matrix products, head_scores(): jnp.einsum('qd,kd->qk', query_h, keys_h, preferred_element_type=jnp.float32)  14.9 us
    unnamed x38, local copies, waits for them, and re-layouts  11.6 us
  transfers between devices with their start and end apart: 5, of which 5 were waited for; matrix products, arithmetic and copies ran while one was open for 12% of the time, Pallas kernels for 0%

commit v1 on v0

v1 whole, which is shorter than its diff:
```python
import jax
import jax.numpy as jnp
from jax import lax
from jax.experimental import pallas as pl
from jax.experimental.pallas import tpu as pltpu
from jax.sharding import Mesh, PartitionSpec as P


HEAD_DIM = 64
NZ, NX, NY = 8, 4, 4
X = ("xh", "xl")
Q_TILE = 256
K_TILE = 256


F32 = jnp.float32
BF16 = jnp.bfloat16
MIB = 1 << 20


def vmem_specs(n):
    return [pl.BlockSpec(memory_space=pltpu.VMEM) for _ in range(n)]


def shift(block, axis, n, by):
    return lax.ppermute(block, axis, [(i, (i + by) % n) for i in range(n)])


def pack_kernel(in_ref, o_ref):
    for i in range(3):
        t = in_ref[i].T
        heads = t.shape[0] // HEAD_DIM
        o_ref[:, i * HEAD_DIM:(i + 1) * HEAD_DIM, :] = t.reshape(heads, HEAD_DIM, t.shape[1])


def pack(query, keys, values):
    rows, width = query.shape[1:]
    return pl.pallas_call(
        pack_kernel,
        out_shape=jax.ShapeDtypeStruct((width // HEAD_DIM, 3 * HEAD_DIM, rows), query.dtype),
        in_specs=vmem_specs(1),
        out_specs=pl.BlockSpec(memory_space=pltpu.VMEM),
        compiler_params=pltpu.CompilerParams(vmem_limit_bytes=4 * MIB),
        name="pack",
    )(jnp.concatenate([query, keys, values], axis=0))


def lanes(refs, lower, upper):
    return jnp.concatenate([ref[z, lower:upper, :] for ref in refs for z in range(ref.shape[0])], axis=1)


def block_steps(q_t, kv_refs, first, s_ref, p_ref, peak_old, emit):
    keys = lanes(kv_refs, first, first + HEAD_DIM).T
    v_t = lanes(kv_refs, first + HEAD_DIM, first + 2 * HEAD_DIM)
    v_aug = jnp.concatenate([v_t, jnp.ones((16, v_t.shape[1]), v_t.dtype)], axis=0)
    n = keys.shape[0]
    tiles = q_t.shape[1] // Q_TILE
    peaks = {}
    for step in range(tiles + 2):
        high = acc = None
        for lower in range(0, n, K_TILE):
            part = slice(lower, lower + K_TILE)
            if step < tiles:
                tile = slice(step * Q_TILE, (step + 1) * Q_TILE)
                s = jnp.dot(keys[part], q_t[:, tile], preferred_element_type=F32)
                s_ref[step % 2, part, :] = s
                top = jnp.max(s.reshape(K_TILE // 8, 8, Q_TILE), axis=0)
                high = top if high is None else jnp.maximum(high, top)
            if 0 <= step - 1 < tiles:
                expo = jnp.exp(s_ref[(step - 1) % 2, part, :] - peaks[step - 1])
                p_ref[(step - 1) % 2, part, :] = expo.astype(BF16)
            if 0 <= step - 2 < tiles:
                summed = jnp.dot(v_aug[:, part], p_ref[step % 2, part, :], preferred_element_type=F32)
                acc = summed if acc is None else acc + summed
        if step < tiles:
            peak = jnp.max(high, axis=0, keepdims=True)
            if peak_old is not None:
                peak = jnp.maximum(peak, peak_old[:, step * Q_TILE:(step + 1) * Q_TILE])
            peaks[step] = peak
        if step >= 2:
            emit(step - 2, peaks.pop(step - 2), acc)


def first_kernel(r_ref, peak_ref, acc_ref, s_ref, p_ref):
    def emit(tile, peak, acc):
        at = slice(tile * Q_TILE, (tile + 1) * Q_TILE)
        peak_ref[:, at] = peak
        acc_ref[:, at] = acc

    block_steps(lanes([r_ref], 0, HEAD_DIM), [r_ref], HEAD_DIM, s_ref, p_ref, None, emit)


def next_kernel(last, n_kv, r_ref, peak_ref, acc_ref, *refs):
    kv_refs, outs, (s_ref, p_ref) = refs[:n_kv], refs[n_kv:-2], refs[-2:]

    def emit(tile, peak, acc):
        at = slice(tile * Q_TILE, (tile + 1) * Q_TILE)
        acc = acc + acc_ref[:, at] * jnp.exp(peak_ref[:, at] - peak)
        if last:
            ctx = (acc[:HEAD_DIM] / acc[HEAD_DIM:HEAD_DIM + 1]).astype(BF16)
            rows = outs[0].shape[3]
            for j in range(Q_TILE // rows):
                for twin in range(2):
                    outs[0][tile * (Q_TILE // rows) + j, twin] = ctx[:, j * rows:(j + 1) * rows]
        else:
            outs[0][:, at] = peak
            outs[1][:, at] = acc

    block_steps(lanes([r_ref], 0, HEAD_DIM), kv_refs, 0, s_ref, p_ref, peak_ref[...], emit)


def attend_scratch(n):
    return [pltpu.VMEM((2, n, Q_TILE), F32), pltpu.VMEM((2, n, Q_TILE), BF16)]


def attend_first(r):
    n = r.shape[0] * r.shape[2]
    return pl.pallas_call(
        first_kernel,
        out_shape=(jax.ShapeDtypeStruct((1, n), F32), jax.ShapeDtypeStruct((HEAD_DIM + 16, n), F32)),
        in_specs=vmem_specs(1),
        out_specs=tuple(vmem_specs(2)),
        scratch_shapes=attend_scratch(n),
        compiler_params=pltpu.CompilerParams(vmem_limit_bytes=16 * MIB),
        name="attend_first",
    )(r)


def attend_next(r, kvs, peak, acc, last):
    n = r.shape[0] * r.shape[2]
    if last:
        shapes = (jax.ShapeDtypeStruct((r.shape[0], 2, HEAD_DIM, r.shape[2]), BF16),)
    else:
        shapes = (jax.ShapeDtypeStruct((1, n), F32), jax.ShapeDtypeStruct((HEAD_DIM + 16, n), F32))
    return pl.pallas_call(
        lambda *refs: next_kernel(last, len(kvs), *refs),
        out_shape=shapes,
        in_specs=vmem_specs(3 + len(kvs)),
        out_specs=tuple(vmem_specs(len(shapes))),
        scratch_shapes=attend_scratch(n),
        compiler_params=pltpu.CompilerParams(vmem_limit_bytes=16 * MIB),
        name="attend_last" if last else "attend_next",
    )(r, peak, acc, *kvs)


def unpack_kernel(at_ref, c_ref, o_ref):
    heads, _, dim, rows = c_ref.shape
    o_ref[0] = c_ref[:, at_ref[1] % 2].reshape(heads * dim, rows).T


def unpack(at, ctx_t):
    heads, _, dim, rows = ctx_t.shape
    return pl.pallas_call(
        unpack_kernel,
        out_shape=jax.ShapeDtypeStruct((1, rows, heads * dim), ctx_t.dtype),
        in_specs=[pl.BlockSpec(memory_space=pltpu.SMEM)] + vmem_specs(1),
        out_specs=pl.BlockSpec(memory_space=pltpu.VMEM),
        compiler_params=pltpu.CompilerParams(vmem_limit_bytes=4 * MIB),
        name="unpack",
    )(at, ctx_t)


def gather_rows(own):
    up = down = own
    pieces = [(own, 0)]
    for j in (1, 2, 3, 4):
        up = shift(up, "z", NZ, 1)
        pieces.append((up, j))
        if j < 4:
            down = shift(down, "z", NZ, -1)
            pieces.append((down, NZ - j))
    return pieces


def project_kernel(behind, at_ref, *refs):
    c0, c1, c3, c2a, c2b = refs[:5]
    ws = refs[5:5 + len(behind)]
    mine_ref, other_ref, ctx_ref, acc_ref = refs[5 + len(behind):]
    z, x, y = at_ref[0], at_ref[1], at_ref[2]
    _, _, dim, rows = c0.shape
    for d, parts in ((0, (c0,)), (1, (c1,)), (3, (c3,)), (2, (c2a, c2b))):
        group = (y + NY - d) % NY
        first = 0
        for part in parts:
            size = part.shape[0] * dim
            for twin in range(2):
                ctx_ref[group, first:first + size, twin * rows:(twin + 1) * rows] = part[:, twin].reshape(size, rows)
            first += size
    acc_ref[...] = jnp.zeros(acc_ref.shape, F32)
    strip = acc_ref.shape[2]
    for dz, w_ref in zip(behind, ws):
        zs = (z + NZ - dz) % NZ
        part = jnp.dot(w_ref[...].reshape(2 * strip, w_ref.shape[2]), ctx_ref[zs // 2], preferred_element_type=F32)
        acc_ref[zs % 2, x // 2] += part[:strip]
        acc_ref[zs % 2, 1 - x // 2] += part[strip:]
    for half in range(2):
        for i in range(2):
            left, right = acc_ref[half, i, :, :rows], acc_ref[half, i, :, rows:]
            second = x % 2 == 1
            mine_ref[half, i] = jnp.where(second, right, left)
            other_ref[half, i] = jnp.where(second, left, right).astype(BF16)


def project(at, contexts, pieces):
    behind = [dz for _, dz in pieces]
    rows = contexts[0].shape[3]
    strip = pieces[0][0].shape[1]
    return pl.pallas_call(
        lambda *refs: project_kernel(behind, *refs),
        out_shape=(
            jax.ShapeDtypeStruct((2, 2, strip, rows), F32),
            jax.ShapeDtypeStruct((2, 2, strip, rows), BF16),
        ),
        in_specs=[pl.BlockSpec(memory_space=pltpu.SMEM)] + vmem_specs(len(contexts) + len(pieces)),
        out_specs=tuple(vmem_specs(2)),
        scratch_shapes=[
            pltpu.VMEM((NY, 8 * HEAD_DIM, 2 * rows), BF16),
            pltpu.VMEM((2, 2, strip, 2 * rows), F32),
        ],
        compiler_params=pltpu.CompilerParams(vmem_limit_bytes=16 * MIB),
        name="project",
    )(at, *contexts, *[p[0] for p in pieces])


def add_kernel(strip, at_ref, mine_ref, other_ref, hidden_ref, o_ref, full_ref):
    second = at_ref[1] % 2
    for half in range(2):
        for x in range(NX):
            first = (half * NX + x) * strip
            mine, other = mine_ref[half, x // 2], other_ref[half, x // 2].astype(F32)
            full_ref[first:first + strip, :] = jnp.where(second == x % 2, mine, other)[:strip]
    o_ref[0] = (hidden_ref[0].astype(F32) + full_ref[...]).astype(o_ref.dtype)


def add_up(at, mine, other, hidden_t, strip):
    return pl.pallas_call(
        lambda *refs: add_kernel(strip, *refs),
        out_shape=jax.ShapeDtypeStruct(hidden_t.shape, hidden_t.dtype),
        in_specs=[pl.BlockSpec(memory_space=pltpu.SMEM)] + vmem_specs(3),
        out_specs=pl.BlockSpec(memory_space=pltpu.VMEM),
        scratch_shapes=[pltpu.VMEM(hidden_t.shape[1:], F32)],
        compiler_params=pltpu.CompilerParams(vmem_limit_bytes=8 * MIB),
        name="add_up",
    )(at, mine, other, hidden_t)


def layer(hidden, query, keys, values, w_out):
    at = jnp.stack([lax.axis_index("z"), lax.axis_index(X), lax.axis_index("mp")]).astype(jnp.int32)
    strip = w_out.shape[1]
    route = [
        ((s * NZ + z) * NY + y, ((1 - s) * NZ + 2 * y + z % 2) * NY + z // 2)
        for s in range(2) for z in range(NZ) for y in range(NY)
    ]
    here = lax.ppermute(w_out[0], ("section", "z", "mp"), route)
    here = jnp.pad(here, ((0, -strip % 8), (0, 0)))
    there = shift(here, X, NX, 2)
    pieces = gather_rows(jnp.stack([here, there]))
    hidden_t = lax.ppermute(jnp.swapaxes(hidden, 1, 2), "section", [(0, 1), (1, 0)])

    packed = pack(query, keys, values)
    r = lax.all_to_all(packed, "z", 0, 0, tiled=True)
    kv = r[:, HEAD_DIM:, :]
    half = NZ // 2
    kv1 = shift(kv, X, NX, 1)
    kv3 = shift(kv, X, NX, -1)
    kv2a = shift(kv1[:half], X, NX, 1)
    kv2b = shift(kv3[half:], X, NX, -1)
    peak, acc = attend_first(r)
    for j, kvs in enumerate(((kv1,), (kv3,), (kv2a, kv2b))):
        out = attend_next(r, kvs, peak, acc, j == 2)
        if j < 2:
            peak, acc = out

    sent = out[0].reshape((2 * NZ,) + out[0].shape[2:])
    own = lax.all_to_all(sent, ("z", "xl"), 0, 0, tiled=True).reshape(out[0].shape)

    def turned(by):
        turn = [(s * NY + y, (1 - s) * NY + (y + by) % NY) for s in range(2) for y in range(NY)]
        return lax.ppermute(own, ("section", "mp"), turn)

    ctx1 = turned(1)
    ctx3 = turned(-1)
    ctx0 = turned(0)
    ctx2a = shift(ctx1[:half], "mp", NY, 1)
    ctx2b = shift(ctx3[half:], "mp", NY, -1)
    context = unpack(at, own)
    mine, other = project(at, (ctx0, ctx1, ctx3, ctx2a, ctx2b), pieces)
    other = lax.ppermute(other, "xl", [(0, 1), (1, 0)])
    handed_t = add_up(at, mine, other, hidden_t, strip)
    return jnp.swapaxes(handed_t, 1, 2), context


def solution(mesh):
    split = Mesh(mesh.devices.reshape(2, NZ, NX // 2, 2, NY), ("section", "z") + X + ("mp",))
    spec = P("section", ("z",) + X, "mp")
    return jax.shard_map(layer, mesh=split, in_specs=(spec,) * 5, out_specs=(spec, spec), check_vma=False)
```

time: 322 us -> 107 us (0.33)
  waiting for transfers between devices: 250 us -> 36.3 us
  starting transfers between devices: 2.5 us -> 52.3 us
  matrix products: 39.4 us -> 0 us
  Pallas kernels: 0 us -> 13.3 us
  between operations: 14 us -> 0.75 us
  local copies, waits for them, and re-layouts: 11.6 us -> 1.39 us
  other arithmetic: 4.54 us -> 1.18 us
    all_gather x3 -> x0, waiting for transfers between devices: 225 us -> none  [the longest x1 88.1 us: body(): lax.all_gather(out_local, 'ctx', axis=0, tiled=True)]
    dot_general x17 -> x0, matrix products: 39.4 us -> none  [the longest x8 18.3 us: body(): jnp.dot(expo.astype(jnp.bfloat16), values_all[:, lower:upper], preferred_...]
    ppermute x1 -> x20, starting transfers between devices: 2.35 us -> 36.4 us  [the longest x14 29.2 us: shift(): return lax.ppermute(block, axis, [(i, (i + by) % n) for i in range(n)])]
    ppermute x1 -> x20, waiting for transfers between devices: 0.43 us -> 27 us  [the longest x14 17.6 us: shift(): return lax.ppermute(block, axis, [(i, (i + by) % n) for i in range(n)])]
    reduce_scatter x1 -> x0, waiting for transfers between devices: 23.2 us -> none  [body(): lax.psum_scatter(branch_terms.astype(jnp.bfloat16), 'mp', scatter_dimensi...]
    all_to_all x0 -> x2, starting transfers between devices: none -> 16 us  [the longest x1 9.13 us: layer(): r = lax.all_to_all(packed, 'z', 0, 0, tiled=True)]
    pallas_call x0 -> x8, Pallas kernels: none -> 13.3 us  [the longest x3 5.58 us: attend_next(): pl.pallas_call(lambda *refs: next_kernel(last, len(kvs), *refs), out_shap...]
    unnamed x38 -> x2, local copies, waits for them, and re-layouts: 11.6 us -> 0.01 us
  transfers between devices with their start and end apart: 5 -> 22, of which waited for: 5 -> 8; matrix products, arithmetic and copies ran while one was open for 12% -> 1% of each run, Pallas kernels for 0% -> 10%
where the time goes in v1:
time: 107 us; the launch traced here: 105 us
  starting transfers between devices  52.3 us (49%)
  waiting for transfers between devices  36.3 us (34%)
  Pallas kernels  13.3 us (12%)
  local copies, waits for them, and re-layouts  1.39 us (1%)
  other arithmetic  1.18 us (1%)
    ppermute x14, starting transfers between devices, shift(): return lax.ppermute(block, axis, [(i, (i + by) % n) for i in range(n)])  29.2 us
    ppermute x14, waiting for transfers between devices, shift(): return lax.ppermute(block, axis, [(i, (i + by) % n) for i in range(n)])  17.6 us
    all_to_all x1, waiting for transfers between devices, layer(): r = lax.all_to_all(packed, 'z', 0, 0, tiled=True)  9.34 us
    all_to_all x1, starting transfers between devices, layer(): r = lax.all_to_all(packed, 'z', 0, 0, tiled=True)  9.13 us
    all_to_all x1, starting transfers between devices, layer(): lax.all_to_all(sent, ('z', 'xl'), 0, 0, tiled=True).reshape(out[0].shape)  6.85 us
    ppermute x3, waiting for transfers between devices, turned(): return lax.ppermute(own, ('section', 'mp'), turn)  6.45 us
    pallas_call x3, Pallas kernels, attend_next(): pl.pallas_call(lambda *refs: next_kernel(last, len(kvs), *refs), out_shap...  5.58 us
    ppermute x3, starting transfers between devices, turned(): return lax.ppermute(own, ('section', 'mp'), turn)  4.83 us
  transfers between devices with their start and end apart: 22, of which 8 were waited for; matrix products, arithmetic and copies ran while one was open for 1% of the time, Pallas kernels for 10%

profile of v1, /device:TPU:1, one launch (start us, length us, event | category | flops | bytes accessed | tf_op | source)
XLA Modules:
  0.0 105.2 jit_solution(16350387312926336780)
XLA Ops:
  2.6 9.1 %all-to-all-start = ((bf16[8,192,128]{2,1,0:T(8,128)(2,1)}), bf16[8,192,128]{2,1,0:T(8,128)(2,1)S(1)}, u32[]{:S(2)}, u32[]{:S(2)}) async-start(bf16[8,192,128]{2,1,0:T(8,128)(2,1)} %pack.1), calls=%async_computation | async-start | bytes 786432 | tf_op jit(solution)/shard_map/all_to_all | solution.py:261
  13.9 2.8 %collective-permute-start.10 = (bf16[152,512]{1,0:T(8,128)(2,1)S(1)}, bf16[152,512]{1,0:T(8,128)(2,1)S(1)}, u32[]{:S(2)}, u32[]{:S(2)}) collective-permute-start(bf16[152,512]{1,0:T(8,128)(2,1)S(1)} %get-tuple-element.19), channel_id=1, source_target_pairs={{0,8},{4,12},{8,0},{12,4},{1,9},{5,13},{9,1},{13,5},{2,10},{6,14},... | collective-permute-start | bytes 466952 | tf_op jit(solution)/shard_map/ppermute | solution.py:26
  16.7 9.3 %all-to-all-done.r_ref.refs_0_ = bf16[8,192,128]{2,1,0:T(8,128)(2,1)S(1)} async-done(((bf16[8,192,128]{2,1,0:T(8,128)(2,1)}), bf16[8,192,128]{2,1,0:T(8,128)(2,1)S(1)}, u32[]{:S(2)}, u32[]{:S(2)}) %all-to-all-start) | async-done | bytes 393248 | tf_op jit(solution)/shard_map/all_to_all | solution.py:261
  27.3 1.5 %collective-permute-start.1 = (bf16[8,128,128]{2,1,0:T(8,128)(2,1)S(1)}, bf16[8,128,128]{2,1,0:T(8,128)(2,1)S(1)}, u32[]{:S(2)}, u32[]{:S(2)}) collective-permute-start(bf16[8,128,128]{2,1,0:T(8,128)(2,1)S(1)} %slice.20), channel_id=1, source_target_pairs={{0,12},{4,0},{8,4},{12,8},{1,13},{5,1},{9,5},{13,9},{2,14},{6,2},{... | collective-permute-start | bytes 786440 | tf_op jit(solution)/shard_map/ppermute | solution.py:26
  28.9 13.1 %collective-permute-start.12 = (bf16[2,152,512]{2,1,0:T(8,128)(2,1)S(1)}, bf16[2,152,512]{2,1,0:T(8,128)(2,1)S(1)}, u32[]{:S(2)}, u32[]{:S(2)}) collective-permute-start(bf16[2,152,512]{2,1,0:T(8,128)(2,1)S(1)} %pad_maximum_fusion.1.refs_6_), channel_id=1, source_target_pairs={{0,112},{16,0},{32,16},{48,32},{64,48},{80,64},{96,80},{112,96},{1... | collective-permute-start | bytes 933896 | tf_op jit(solution)/shard_map/ppermute | solution.py:26
  42.0 1.3 %collective-permute-start.2 = (bf16[4,128,128]{2,1,0:T(8,128)(2,1)S(1)}, bf16[4,128,128]{2,1,0:T(8,128)(2,1)S(1)}, u32[]{:S(2)}, u32[]{:S(2)}) collective-permute-start(bf16[4,128,128]{2,1,0:T(8,128)(2,1)S(1)} %slice.21), channel_id=1, source_target_pairs={{0,4},{4,8},{8,12},{12,0},{1,5},{5,9},{9,13},{13,1},{2,6},{6,10},{... | collective-permute-start | bytes 393224 | tf_op jit(solution)/shard_map/ppermute | solution.py:26
  43.4 1.5 %collective-permute-start.3 = (bf16[4,128,128]{2,1,0:T(8,128)(2,1)S(1)}, bf16[4,128,128]{2,1,0:T(8,128)(2,1)S(1)}, u32[]{:S(2)}, u32[]{:S(2)}) collective-permute-start(bf16[4,128,128]{2,1,0:T(8,128)(2,1)S(1)} %slice.22), channel_id=1, source_target_pairs={{0,12},{4,0},{8,4},{12,8},{1,13},{5,1},{9,5},{13,9},{2,14},{6,2},{... | collective-permute-start | bytes 393224 | tf_op jit(solution)/shard_map/ppermute | solution.py:26
  44.9 4.1 %collective-permute-done.11.refs_7_ = bf16[2,152,512]{2,1,0:T(8,128)(2,1)S(1)} collective-permute-done((bf16[2,152,512]{2,1,0:T(8,128)(2,1)S(1)}, bf16[2,152,512]{2,1,0:T(8,128)(2,1)S(1)}, u32[]{:S(2)}, u32[]{:S(2)}) %collective-permute-start.11) | collective-permute-done | bytes 311328 | tf_op jit(solution)/shard_map/ppermute | solution.py:26
  48.9 1.6 %attend_first.1 = (f32[1,1024]{1,0:T(1,128)S(1)}, f32[80,1024]{1,0:T(8,128)S(1)}) custom-call(bf16[8,192,128]{2,1,0:T(8,128)(2,1)S(1)} %all-to-all-done.r_ref.refs_0_), custom_call_target="tpu_custom_call" | custom-call | tf_op jit(solution)/shard_map/attend_first/pallas_call | solution.py:118
  50.6 1.6 %attend_next.2 = (f32[1,1024]{1,0:T(1,128)S(1)}, f32[80,1024]{1,0:T(8,128)S(1)}) custom-call(bf16[8,192,128]{2,1,0:T(8,128)(2,1)S(1)} %all-to-all-done.r_ref.refs_0_, f32[1,1024]{1,0:T(1,128)S(1)} %get-tuple-element.10.refs_1_, f32[80,1024]{1,0:T(8,128)S(1)} %get-tuple-element.11.refs_2_, bf16[8,128,128]{2,1,0:T(8,128)(2,1)S(1)} %collective-permute-done.refs_3_), custom_call_target="tpu_custom_call" | custom-call | tf_op jit(solution)/shard_map/attend_next/pallas_call | solution.py:135
  52.2 1.6 %attend_next.3 = (f32[1,1024]{1,0:T(1,128)S(1)}, f32[80,1024]{1,0:T(8,128)S(1)}) custom-call(bf16[8,192,128]{2,1,0:T(8,128)(2,1)S(1)} %all-to-all-done.r_ref.refs_0_, f32[1,1024]{1,0:T(1,128)S(1)} %get-tuple-element.12.refs_1_, f32[80,1024]{1,0:T(8,128)S(1)} %get-tuple-element.13.refs_2_, bf16[8,128,128]{2,1,0:T(8,128)(2,1)S(1)} %collective-permute-done.1.refs_3_), custom_call_target="tpu_custom_call" | custom-call | tf_op jit(solution)/shard_map/attend_next/pallas_call | solution.py:135
  53.8 2.4 %attend_last.1 = bf16[8,2,64,128]{3,2,1,0:T(8,128)(2,1)} custom-call(bf16[8,192,128]{2,1,0:T(8,128)(2,1)S(1)} %all-to-all-done.r_ref.refs_0_, f32[1,1024]{1,0:T(1,128)S(1)} %get-tuple-element.14.refs_1_, f32[80,1024]{1,0:T(8,128)S(1)} %get-tuple-element.15.refs_2_, bf16[4,128,128]{2,1,0:T(8,128)(2,1)S(1)} %collective-permute-done.2.refs_3_, ...), custom_call_target="tpu_custom_call" | custom-call | tf_op jit(solution)/shard_map/attend_last/pallas_call | solution.py:135
  56.2 6.9 %all-to-all-start.1 = ((bf16[16,64,128]{2,1,0:T(8,128)(2,1)}), bf16[16,64,128]{2,1,0:T(8,128)(2,1)S(1)}, u32[]{:S(2)}, u32[]{:S(2)}) async-start(bf16[16,64,128]{2,1,0:T(8,128)(2,1)} %bitcast.3), calls=%async_computation.1 | async-start | bytes 524288 | tf_op jit(solution)/shard_map/all_to_all | solution.py:275
  63.0 2.7 %collective-permute-start.14 = (bf16[2,152,512]{2,1,0:T(8,128)(2,1)S(1)}, bf16[2,152,512]{2,1,0:T(8,128)(2,1)S(1)}, u32[]{:S(2)}, u32[]{:S(2)}) collective-permute-start(bf16[2,152,512]{2,1,0:T(8,128)(2,1)S(1)} %collective-permute-done.12.refs_8_), channel_id=1, source_target_pairs={{0,112},{16,0},{32,16},{48,32},{64,48},{80,64},{96,80},{112,96},{1... | collective-permute-start | bytes 933896 | tf_op jit(solution)/shard_map/ppermute | solution.py:26
  65.7 10.7 %collective-permute-done.14.refs_10_ = bf16[2,152,512]{2,1,0:T(8,128)(2,1)S(1)} collective-permute-done((bf16[2,152,512]{2,1,0:T(8,128)(2,1)S(1)}, bf16[2,152,512]{2,1,0:T(8,128)(2,1)S(1)}, u32[]{:S(2)}, u32[]{:S(2)}) %collective-permute-start.14) | collective-permute-done | bytes 311328 | tf_op jit(solution)/shard_map/ppermute | solution.py:26
  76.4 2.3 %collective-permute-start.16 = (bf16[2,152,512]{2,1,0:T(8,128)(2,1)S(1)}, bf16[2,152,512]{2,1,0:T(8,128)(2,1)S(1)}, u32[]{:S(2)}, u32[]{:S(2)}) collective-permute-start(bf16[2,152,512]{2,1,0:T(8,128)(2,1)S(1)} %collective-permute-done.14.refs_10_), channel_id=1, source_target_pairs={{0,112},{16,0},{32,16},{48,32},{64,48},{80,64},{96,80},{112,96},{1... | collective-permute-start | bytes 933896 | tf_op jit(solution)/shard_map/ppermute | solution.py:26
  78.7 3.6 %collective-permute-start.5 = (bf16[8,2,64,128]{3,2,1,0:T(8,128)(2,1)S(1)}, bf16[8,2,64,128]{3,2,1,0:T(8,128)(2,1)S(1)}, u32[]{:S(2)}, u32[]{:S(2)}) collective-permute-start(bf16[8,2,64,128]{3,2,1,0:T(8,128)(2,1)S(1)} %bitcast.11), channel_id=1, source_target_pairs={{0,129},{1,130},{2,131},{3,128},{128,1},{129,2},{130,3},{131,0},{4... | collective-permute-start | bytes 786440 | tf_op jit(solution)/shard_map/ppermute | solution.py:279
  83.5 6.4 %collective-permute-done.5.refs_2_ = bf16[8,2,64,128]{3,2,1,0:T(8,128)(2,1)S(1)} collective-permute-done((bf16[8,2,64,128]{3,2,1,0:T(8,128)(2,1)S(1)}, bf16[8,2,64,128]{3,2,1,0:T(8,128)(2,1)S(1)}, u32[]{:S(2)}, u32[]{:S(2)}) %collective-permute-start.5) | collective-permute-done | bytes 262176 | tf_op jit(solution)/shard_map/ppermute | solution.py:279
  91.7 2.3 %collective-permute-start.8 = (bf16[4,2,64,128]{3,2,1,0:T(8,128)(2,1)}, bf16[4,2,64,128]{3,2,1,0:T(8,128)(2,1)S(1)}, u32[]{:S(2)}, u32[]{:S(2)}) collective-permute-start(bf16[4,2,64,128]{3,2,1,0:T(8,128)(2,1)} %slice.24), channel_id=1, source_target_pairs={{0,3},{1,0},{2,1},{3,2},{4,7},{5,4},{6,5},{7,6},{8,11},{9,8},{10,9... | collective-permute-start | bytes 393224 | tf_op jit(solution)/shard_map/ppermute | solution.py:26
  94.1 2.6 %collective-permute-done.7.refs_4_ = bf16[4,2,64,128]{3,2,1,0:T(8,128)(2,1)S(1)} collective-permute-done((bf16[4,2,64,128]{3,2,1,0:T(8,128)(2,1)}, bf16[4,2,64,128]{3,2,1,0:T(8,128)(2,1)S(1)}, u32[]{:S(2)}, u32[]{:S(2)}) %collective-permute-start.7) | collective-permute-done | bytes 131104 | tf_op jit(solution)/shard_map/ppermute | solution.py:26
  96.9 2.1 %project.1 = (f32[2,2,152,128]{3,2,1,0:T(8,128)S(1)}, bf16[2,2,152,128]{3,2,1,0:T(8,128)(2,1)S(1)}) custom-call(s32[3]{0:T(128)S(1)} %pad_add_fusion.refs_0_.at_ref, bf16[8,2,64,128]{3,2,1,0:T(8,128)(2,1)} %collective-permute-done.4.refs_1_, bf16[8,2,64,128]{3,2,1,0:T(8,128)(2,1)S(1)} %collective-permute-done.5.refs_2_, ...), custom_call_target="tpu_custom_call" | custom-call | tf_op jit(solution)/shard_map/project/pallas_call | solution.py:208
  100.2 1.3 %unpack.1 = bf16[1,128,512]{2,1,0:T(8,128)(2,1)} custom-call(s32[3]{0:T(128)S(1)} %pad_add_fusion.refs_0_.at_ref, bf16[8,2,64,128]{3,2,1,0:T(8,128)(2,1)S(1)} %bitcast.14), custom_call_target="tpu_custom_call" | custom-call | tf_op jit(solution)/shard_map/unpack/pallas_call | solution.py:153
  101.5 1.9 %collective-permute-done.18.refs_2_ = bf16[2,2,152,128]{3,2,1,0:T(8,128)(2,1)S(1)} collective-permute-done((bf16[2,2,152,128]{3,2,1,0:T(8,128)(2,1)S(1)}, bf16[2,2,152,128]{3,2,1,0:T(8,128)(2,1)S(1)}, u32[]{:S(2)}, u32[]{:S(2)}) %collective-permute-start.18) | collective-permute-done | bytes 155680 | tf_op jit(solution)/shard_map/ppermute | solution.py:288
  103.4 1.8 %add_up.1 = bf16[1,1168,128]{2,1,0:T(8,128)(2,1)} custom-call(s32[3]{0:T(128)S(1)} %pad_add_fusion.refs_0_.at_ref, f32[2,2,152,128]{3,2,1,0:T(8,128)S(1)} %get-tuple-element.16.refs_1_, bf16[2,2,152,128]{3,2,1,0:T(8,128)(2,1)S(1)} %collective-permute-done.18.refs_2_, bf16[1,1168,128]{2,1,0:T(8,128)(2,1)} %collective-permute-done.19.refs_3_), custom_call_target="tpu_custom_call" | custom-call | tf_op jit(solution)/shard_map/add_up/pallas_call | solution.py:236
  (39 shorter events, 10.1 us)
Async XLA Ops:
  2.6 9.1 %copy-start = (bf16[1,146,512]{2,1,0:T(8,128)(2,1)S(1)}, bf16[1,146,512]{2,1,0:T(8,128)(2,1)}, u32[]{:S(2)}) copy-start(bf16[1,146,512]{2,1,0:T(8,128)(2,1)} %param.9) | copy-start | bytes 448516
  2.6 23.4 %all-to-all-start = ((bf16[8,192,128]{2,1,0:T(8,128)(2,1)}), bf16[8,192,128]{2,1,0:T(8,128)(2,1)S(1)}, u32[]{:S(2)}, u32[]{:S(2)}) async-start(bf16[8,192,128]{2,1,0:T(8,128)(2,1)} %pack.1), calls=%async_computation | async-start | bytes 786432 | tf_op jit(solution)/shard_map/all_to_all | solution.py:261
  11.8 2.1 %collective-permute-start.9 = (bf16[146,512]{1,0:T(8,128)(2,1)S(1)}, bf16[146,512]{1,0:T(8,128)(2,1)S(1)}, u32[]{:S(2)}, u32[]{:S(2)}) collective-permute-start(bf16[146,512]{1,0:T(8,128)(2,1)S(1)} %bitcast.18), channel_id=1, source_target_pairs={{0,128},{1,160},{2,192},{3,224},{16,144},{17,176},{18,208},{19,240... | collective-permute-start | bytes 448520 | tf_op jit(solution)/shard_map/ppermute | solution.py:254
  13.9 15.0 %collective-permute-start.10 = (bf16[152,512]{1,0:T(8,128)(2,1)S(1)}, bf16[152,512]{1,0:T(8,128)(2,1)S(1)}, u32[]{:S(2)}, u32[]{:S(2)}) collective-permute-start(bf16[152,512]{1,0:T(8,128)(2,1)S(1)} %get-tuple-element.19), channel_id=1, source_target_pairs={{0,8},{4,12},{8,0},{12,4},{1,9},{5,13},{9,1},{13,5},{2,10},{6,14},... | collective-permute-start | bytes 466952 | tf_op jit(solution)/shard_map/ppermute | solution.py:26
  26.0 16.0 %collective-permute-start = (bf16[8,128,128]{2,1,0:T(8,128)(2,1)S(1)}, bf16[8,128,128]{2,1,0:T(8,128)(2,1)S(1)}, u32[]{:S(2)}, u32[]{:S(2)}) collective-permute-start(bf16[8,128,128]{2,1,0:T(8,128)(2,1)S(1)} %slice.20), channel_id=1, source_target_pairs={{0,4},{4,8},{8,12},{12,0},{1,5},{5,9},{9,13},{13,1},{2,6},{6,10},{... | collective-permute-start | bytes 786440 | tf_op jit(solution)/shard_map/ppermute | solution.py:26
  27.3 16.0 %collective-permute-start.1 = (bf16[8,128,128]{2,1,0:T(8,128)(2,1)S(1)}, bf16[8,128,128]{2,1,0:T(8,128)(2,1)S(1)}, u32[]{:S(2)}, u32[]{:S(2)}) collective-permute-start(bf16[8,128,128]{2,1,0:T(8,128)(2,1)S(1)} %slice.20), channel_id=1, source_target_pairs={{0,12},{4,0},{8,4},{12,8},{1,13},{5,1},{9,5},{13,9},{2,14},{6,2},{... | collective-permute-start | bytes 786440 | tf_op jit(solution)/shard_map/ppermute | solution.py:26
  28.8 20.1 %collective-permute-start.11 = (bf16[2,152,512]{2,1,0:T(8,128)(2,1)S(1)}, bf16[2,152,512]{2,1,0:T(8,128)(2,1)S(1)}, u32[]{:S(2)}, u32[]{:S(2)}) collective-permute-start(bf16[2,152,512]{2,1,0:T(8,128)(2,1)S(1)} %pad_maximum_fusion.1.refs_6_), channel_id=1, source_target_pairs={{0,16},{16,32},{32,48},{48,64},{64,80},{80,96},{96,112},{112,0},{1... | collective-permute-start | bytes 933896 | tf_op jit(solution)/shard_map/ppermute | solution.py:26
  28.9 34.1 %collective-permute-start.12 = (bf16[2,152,512]{2,1,0:T(8,128)(2,1)S(1)}, bf16[2,152,512]{2,1,0:T(8,128)(2,1)S(1)}, u32[]{:S(2)}, u32[]{:S(2)}) collective-permute-start(bf16[2,152,512]{2,1,0:T(8,128)(2,1)S(1)} %pad_maximum_fusion.1.refs_6_), channel_id=1, source_target_pairs={{0,112},{16,0},{32,16},{48,32},{64,48},{80,64},{96,80},{112,96},{1... | collective-permute-start | bytes 933896 | tf_op jit(solution)/shard_map/ppermute | solution.py:26
  42.0 11.8 %collective-permute-start.2 = (bf16[4,128,128]{2,1,0:T(8,128)(2,1)S(1)}, bf16[4,128,128]{2,1,0:T(8,128)(2,1)S(1)}, u32[]{:S(2)}, u32[]{:S(2)}) collective-permute-start(bf16[4,128,128]{2,1,0:T(8,128)(2,1)S(1)} %slice.21), channel_id=1, source_target_pairs={{0,4},{4,8},{8,12},{12,0},{1,5},{5,9},{9,13},{13,1},{2,6},{6,10},{... | collective-permute-start | bytes 393224 | tf_op jit(solution)/shard_map/ppermute | solution.py:26
  43.4 10.4 %collective-permute-start.3 = (bf16[4,128,128]{2,1,0:T(8,128)(2,1)S(1)}, bf16[4,128,128]{2,1,0:T(8,128)(2,1)S(1)}, u32[]{:S(2)}, u32[]{:S(2)}) collective-permute-start(bf16[4,128,128]{2,1,0:T(8,128)(2,1)S(1)} %slice.22), channel_id=1, source_target_pairs={{0,12},{4,0},{8,4},{12,8},{1,13},{5,1},{9,5},{13,9},{2,14},{6,2},{... | collective-permute-start | bytes 393224 | tf_op jit(solution)/shard_map/ppermute | solution.py:26
  48.9 16.8 %collective-permute-start.13 = (bf16[2,152,512]{2,1,0:T(8,128)(2,1)S(1)}, bf16[2,152,512]{2,1,0:T(8,128)(2,1)S(1)}, u32[]{:S(2)}, u32[]{:S(2)}) collective-permute-start(bf16[2,152,512]{2,1,0:T(8,128)(2,1)S(1)} %collective-permute-done.11.refs_7_), channel_id=1, source_target_pairs={{0,16},{16,32},{32,48},{48,64},{64,80},{80,96},{96,112},{112,0},{1... | collective-permute-start | bytes 933896 | tf_op jit(solution)/shard_map/ppermute | solution.py:26
  56.2 22.5 %all-to-all-start.1 = ((bf16[16,64,128]{2,1,0:T(8,128)(2,1)}), bf16[16,64,128]{2,1,0:T(8,128)(2,1)S(1)}, u32[]{:S(2)}, u32[]{:S(2)}) async-start(bf16[16,64,128]{2,1,0:T(8,128)(2,1)} %bitcast.3), calls=%async_computation.1 | async-start | bytes 524288 | tf_op jit(solution)/shard_map/all_to_all | solution.py:275
  63.0 13.3 %collective-permute-start.14 = (bf16[2,152,512]{2,1,0:T(8,128)(2,1)S(1)}, bf16[2,152,512]{2,1,0:T(8,128)(2,1)S(1)}, u32[]{:S(2)}, u32[]{:S(2)}) collective-permute-start(bf16[2,152,512]{2,1,0:T(8,128)(2,1)S(1)} %collective-permute-done.12.refs_8_), channel_id=1, source_target_pairs={{0,112},{16,0},{32,16},{48,32},{64,48},{80,64},{96,80},{112,96},{1... | collective-permute-start | bytes 933896 | tf_op jit(solution)/shard_map/ppermute | solution.py:26
  65.7 17.6 %collective-permute-start.15 = (bf16[2,152,512]{2,1,0:T(8,128)(2,1)S(1)}, bf16[2,152,512]{2,1,0:T(8,128)(2,1)S(1)}, u32[]{:S(2)}, u32[]{:S(2)}) collective-permute-start(bf16[2,152,512]{2,1,0:T(8,128)(2,1)S(1)} %collective-permute-done.13.refs_9_), channel_id=1, source_target_pairs={{0,16},{16,32},{32,48},{48,64},{64,80},{80,96},{96,112},{112,0},{1... | collective-permute-start | bytes 933896 | tf_op jit(solution)/shard_map/ppermute | solution.py:26
  76.4 15.3 %collective-permute-start.16 = (bf16[2,152,512]{2,1,0:T(8,128)(2,1)S(1)}, bf16[2,152,512]{2,1,0:T(8,128)(2,1)S(1)}, u32[]{:S(2)}, u32[]{:S(2)}) collective-permute-start(bf16[2,152,512]{2,1,0:T(8,128)(2,1)S(1)} %collective-permute-done.14.refs_10_), channel_id=1, source_target_pairs={{0,112},{16,0},{32,16},{48,32},{64,48},{80,64},{96,80},{112,96},{1... | collective-permute-start | bytes 933896 | tf_op jit(solution)/shard_map/ppermute | solution.py:26
  78.7 11.2 %collective-permute-start.5 = (bf16[8,2,64,128]{3,2,1,0:T(8,128)(2,1)S(1)}, bf16[8,2,64,128]{3,2,1,0:T(8,128)(2,1)S(1)}, u32[]{:S(2)}, u32[]{:S(2)}) collective-permute-start(bf16[8,2,64,128]{3,2,1,0:T(8,128)(2,1)S(1)} %bitcast.11), channel_id=1, source_target_pairs={{0,129},{1,130},{2,131},{3,128},{128,1},{129,2},{130,3},{131,0},{4... | collective-permute-start | bytes 786440 | tf_op jit(solution)/shard_map/ppermute | solution.py:279
  82.2 8.4 %collective-permute-start.6 = (bf16[8,2,64,128]{3,2,1,0:T(8,128)(2,1)S(1)}, bf16[8,2,64,128]{3,2,1,0:T(8,128)(2,1)S(1)}, u32[]{:S(2)}, u32[]{:S(2)}) collective-permute-start(bf16[8,2,64,128]{3,2,1,0:T(8,128)(2,1)S(1)} %bitcast.12), channel_id=1, source_target_pairs={{0,131},{1,128},{2,129},{3,130},{128,3},{129,0},{130,1},{131,2},{4... | collective-permute-start | bytes 786440 | tf_op jit(solution)/shard_map/ppermute | solution.py:279
  83.3 10.8 %collective-permute-start.17 = (bf16[2,152,512]{2,1,0:T(8,128)(2,1)S(1)}, bf16[2,152,512]{2,1,0:T(8,128)(2,1)S(1)}, u32[]{:S(2)}, u32[]{:S(2)}) collective-permute-start(bf16[2,152,512]{2,1,0:T(8,128)(2,1)S(1)} %collective-permute-done.15.refs_11_), channel_id=1, source_target_pairs={{0,16},{16,32},{32,48},{48,64},{64,80},{80,96},{96,112},{112,0},{1... | collective-permute-start | bytes 933896 | tf_op jit(solution)/shard_map/ppermute | solution.py:26
  83.3 10.8 %collective-permute-start.4 = (bf16[8,2,64,128]{3,2,1,0:T(8,128)(2,1)S(1)}, bf16[8,2,64,128]{3,2,1,0:T(8,128)(2,1)}, u32[]{:S(2)}, u32[]{:S(2)}) collective-permute-start(bf16[8,2,64,128]{3,2,1,0:T(8,128)(2,1)S(1)} %bitcast.13), channel_id=1, source_target_pairs={{0,128},{1,129},{2,130},{3,131},{128,0},{129,1},{130,2},{131,3},{4... | collective-permute-start | bytes 786440 | tf_op jit(solution)/shard_map/ppermute | solution.py:279
  89.9 11.6 %collective-permute-start.19 = (bf16[1,1168,128]{2,1,0:T(8,128)(2,1)}, bf16[1,1168,128]{2,1,0:T(8,128)(2,1)}, u32[]{:S(2)}, u32[]{:S(2)}) collective-permute-start(bf16[1,1168,128]{2,1,0:T(8,128)(2,1)} %bitcast.17), channel_id=1, source_target_pairs={{0,128},{128,0},{1,129},{129,1},{2,130},{130,2},{3,131},{131,3},{4... | collective-permute-start | bytes 897032 | tf_op jit(solution)/shard_map/ppermute | solution.py:258
  90.6 6.0 %collective-permute-start.7 = (bf16[4,2,64,128]{3,2,1,0:T(8,128)(2,1)}, bf16[4,2,64,128]{3,2,1,0:T(8,128)(2,1)S(1)}, u32[]{:S(2)}, u32[]{:S(2)}) collective-permute-start(bf16[4,2,64,128]{3,2,1,0:T(8,128)(2,1)} %slice.23), channel_id=1, source_target_pairs={{0,1},{1,2},{2,3},{3,0},{4,5},{5,6},{6,7},{7,4},{8,9},{9,10},{10,1... | collective-permute-start | bytes 393224 | tf_op jit(solution)/shard_map/ppermute | solution.py:26
  91.7 5.2 %collective-permute-start.8 = (bf16[4,2,64,128]{3,2,1,0:T(8,128)(2,1)}, bf16[4,2,64,128]{3,2,1,0:T(8,128)(2,1)S(1)}, u32[]{:S(2)}, u32[]{:S(2)}) collective-permute-start(bf16[4,2,64,128]{3,2,1,0:T(8,128)(2,1)} %slice.24), channel_id=1, source_target_pairs={{0,3},{1,0},{2,1},{3,2},{4,7},{5,4},{6,5},{7,6},{8,11},{9,8},{10,9... | collective-permute-start | bytes 393224 | tf_op jit(solution)/shard_map/ppermute | solution.py:26
  98.9 4.5 %collective-permute-start.18 = (bf16[2,2,152,128]{3,2,1,0:T(8,128)(2,1)S(1)}, bf16[2,2,152,128]{3,2,1,0:T(8,128)(2,1)S(1)}, u32[]{:S(2)}, u32[]{:S(2)}) collective-permute-start(bf16[2,2,152,128]{3,2,1,0:T(8,128)(2,1)S(1)} %get-tuple-element.17), channel_id=1, source_target_pairs={{0,4},{4,0},{1,5},{5,1},{2,6},{6,2},{3,7},{7,3},{8,12},{12,8},{9,1... | collective-permute-start | bytes 466952 | tf_op jit(solution)/shard_map/ppermute | solution.py:288

commit v2 on v1

--- a/solution.py
+++ b/solution.py
@@ -173,12 +173,12 @@
 
 
 def project_kernel(behind, at_ref, *refs):
-    c0, c1, c3, c2a, c2b = refs[:5]
-    ws = refs[5:5 + len(behind)]
-    mine_ref, other_ref, ctx_ref, acc_ref = refs[5 + len(behind):]
+    c0, c1a, c1b, c3a, c3b, c2a, c2b = refs[:7]
+    ws = refs[7:-4]
+    mine_ref, other_ref, ctx_ref, acc_ref = refs[-4:]
     z, x, y = at_ref[0], at_ref[1], at_ref[2]
     _, _, dim, rows = c0.shape
-    for d, parts in ((0, (c0,)), (1, (c1,)), (3, (c3,)), (2, (c2a, c2b))):
+    for d, parts in ((0, (c0,)), (1, (c1a, c1b)), (3, (c3a, c3b)), (2, (c2a, c2b))):
         group = (y + NY - d) % NY
         first = 0
         for part in parts:
@@ -259,14 +259,16 @@
 
     packed = pack(query, keys, values)
     r = lax.all_to_all(packed, "z", 0, 0, tiled=True)
-    kv = r[:, HEAD_DIM:, :]
     half = NZ // 2
-    kv1 = shift(kv, X, NX, 1)
-    kv3 = shift(kv, X, NX, -1)
-    kv2a = shift(kv1[:half], X, NX, 1)
-    kv2b = shift(kv3[half:], X, NX, -1)
+    low, high = r[:half, HEAD_DIM:, :], r[half:, HEAD_DIM:, :]
+    kv1a = shift(low, X, NX, 1)
+    kv3b = shift(high, X, NX, -1)
+    kv1b = shift(high, X, NX, 1)
+    kv3a = shift(low, X, NX, -1)
+    kv2a = shift(kv1a, X, NX, 1)
+    kv2b = shift(kv3b, X, NX, -1)
     peak, acc = attend_first(r)
-    for j, kvs in enumerate(((kv1,), (kv3,), (kv2a, kv2b))):
+    for j, kvs in enumerate(((kv1a, kv1b), (kv3a, kv3b), (kv2a, kv2b))):
         out = attend_next(r, kvs, peak, acc, j == 2)
         if j < 2:
             peak, acc = out
@@ -274,17 +276,20 @@
     sent = out[0].reshape((2 * NZ,) + out[0].shape[2:])
     own = lax.all_to_all(sent, ("z", "xl"), 0, 0, tiled=True).reshape(out[0].shape)
 
-    def turned(by):
+    def turned(block, by):
         turn = [(s * NY + y, (1 - s) * NY + (y + by) % NY) for s in range(2) for y in range(NY)]
-        return lax.ppermute(own, ("section", "mp"), turn)
-
-    ctx1 = turned(1)
-    ctx3 = turned(-1)
-    ctx0 = turned(0)
-    ctx2a = shift(ctx1[:half], "mp", NY, 1)
-    ctx2b = shift(ctx3[half:], "mp", NY, -1)
+        return lax.ppermute(block, ("section", "mp"), turn)
+
+    low, high = own[:half], own[half:]
+    ctx1a = turned(low, 1)
+    ctx3b = turned(high, -1)
+    ctx1b = turned(high, 1)
+    ctx3a = turned(low, -1)
+    ctx0 = turned(own, 0)
+    ctx2a = shift(ctx1a, "mp", NY, 1)
+    ctx2b = shift(ctx3b, "mp", NY, -1)
     context = unpack(at, own)
-    mine, other = project(at, (ctx0, ctx1, ctx3, ctx2a, ctx2b), pieces)
+    mine, other = project(at, (ctx0, ctx1a, ctx1b, ctx3a, ctx3b, ctx2a, ctx2b), pieces)
     other = lax.ppermute(other, "xl", [(0, 1), (1, 0)])
     handed_t = add_up(at, mine, other, hidden_t, strip)
     return jnp.swapaxes(handed_t, 1, 2), context

time: 107 us -> 114 us (1.065)
  starting transfers between devices: 52.3 us -> 66.3 us
  waiting for transfers between devices: 36.3 us -> 28 us
    ppermute x14 -> x16, starting transfers between devices: 29.2 us -> 36.3 us  [shift(): return lax.ppermute(block, axis, [(i, (i + by) % n) for i in range(n)])]
    ppermute x3 -> x5, waiting for transfers between devices: 6.45 us -> 0.01 us  [turned(): return lax.ppermute(block, ('section', 'mp'), turn)]
    all_to_all x1, waiting for transfers between devices: 9.34 us -> 3.6 us  [layer(): r = lax.all_to_all(packed, 'z', 0, 0, tiled=True)]
    ppermute x3 -> x5, starting transfers between devices: 4.83 us -> 9.85 us  [turned(): return lax.ppermute(block, ('section', 'mp'), turn)]
    ppermute x14 -> x16, waiting for transfers between devices: 17.6 us -> 21.5 us  [shift(): return lax.ppermute(block, axis, [(i, (i + by) % n) for i in range(n)])]
    ppermute x1, starting transfers between devices: 0.01 us -> 2.97 us  [layer(): lax.ppermute(jnp.swapaxes(hidden, 1, 2), 'section', [(0, 1), (1, 0)])]
    unnamed x2 -> x6, local copies, waits for them, and re-layouts: 0.01 us -> 1.56 us
  transfers between devices with their start and end apart: 22 -> 26, of which waited for: 8 -> 8; matrix products, arithmetic and copies ran while one was open for 1% -> 1% of each run, Pallas kernels for 10% -> 10%
where the time goes in v2:
time: 114 us; the launch traced here: 111 us
  starting transfers between devices  66.3 us (58%)
  waiting for transfers between devices  28 us (25%)
  Pallas kernels  13 us (11%)
  local copies, waits for them, and re-layouts  2.27 us (2%)
  other arithmetic  1.18 us (1%)
    ppermute x16, starting transfers between devices, shift(): return lax.ppermute(block, axis, [(i, (i + by) % n) for i in range(n)])  36.3 us
    ppermute x16, waiting for transfers between devices, shift(): return lax.ppermute(block, axis, [(i, (i + by) % n) for i in range(n)])  21.5 us
    ppermute x5, starting transfers between devices, turned(): return lax.ppermute(block, ('section', 'mp'), turn)  9.85 us
    all_to_all x1, starting transfers between devices, layer(): r = lax.all_to_all(packed, 'z', 0, 0, tiled=True)  9.13 us
    all_to_all x1, starting transfers between devices, layer(): lax.all_to_all(sent, ('z', 'xl'), 0, 0, tiled=True).reshape(out[0].shape)  5.98 us
    pallas_call x3, Pallas kernels, attend_next(): pl.pallas_call(lambda *refs: next_kernel(last, len(kvs), *refs), out_shap...  5.59 us
    all_to_all x1, waiting for transfers between devices, layer(): r = lax.all_to_all(packed, 'z', 0, 0, tiled=True)  3.6 us
    ppermute x1, starting transfers between devices, layer(): lax.ppermute(jnp.swapaxes(hidden, 1, 2), 'section', [(0, 1), (1, 0)])  2.97 us
  transfers between devices with their start and end apart: 26, of which 8 were waited for; matrix products, arithmetic and copies ran while one was open for 1% of the time, Pallas kernels for 10%

profile of v2, /device:TPU:1, one launch (start us, length us, event | category | flops | bytes accessed | tf_op | source)
XLA Modules:
  0.0 111.5 jit_solution(3393714609772563878)
XLA Ops:
  2.6 9.1 %all-to-all-start = ((bf16[8,192,128]{2,1,0:T(8,128)(2,1)}), bf16[8,192,128]{2,1,0:T(8,128)(2,1)S(1)}, u32[]{:S(2)}, u32[]{:S(2)}) async-start(bf16[8,192,128]{2,1,0:T(8,128)(2,1)} %pack.1), calls=%async_computation | async-start | bytes 786432 | tf_op jit(solution)/shard_map/all_to_all | solution.py:261
  13.8 2.8 %collective-permute-start.14 = (bf16[152,512]{1,0:T(8,128)(2,1)S(1)}, bf16[152,512]{1,0:T(8,128)(2,1)S(1)}, u32[]{:S(2)}, u32[]{:S(2)}) collective-permute-start(bf16[152,512]{1,0:T(8,128)(2,1)S(1)} %get-tuple-element.23), channel_id=1, source_target_pairs={{0,8},{4,12},{8,0},{12,4},{1,9},{5,13},{9,1},{13,5},{2,10},{6,14},... | collective-permute-start | bytes 466952 | tf_op jit(solution)/shard_map/ppermute | solution.py:26
  16.7 4.0 %collective-permute-done.14 = bf16[152,512]{1,0:T(8,128)(2,1)S(1)} collective-permute-done((bf16[152,512]{1,0:T(8,128)(2,1)S(1)}, bf16[152,512]{1,0:T(8,128)(2,1)S(1)}, u32[]{:S(2)}, u32[]{:S(2)}) %collective-permute-start.14) | collective-permute-done | bytes 155680 | tf_op jit(solution)/shard_map/ppermute | solution.py:26
  20.7 1.7 %collective-permute-start.15 = (bf16[2,152,512]{2,1,0:T(8,128)(2,1)S(1)}, bf16[2,152,512]{2,1,0:T(8,128)(2,1)S(1)}, u32[]{:S(2)}, u32[]{:S(2)}) collective-permute-start(bf16[2,152,512]{2,1,0:T(8,128)(2,1)S(1)} %pad_maximum_fusion.1.refs_8_), channel_id=1, source_target_pairs={{0,16},{16,32},{32,48},{48,64},{64,80},{80,96},{96,112},{112,0},{1... | collective-permute-start | bytes 933896 | tf_op jit(solution)/shard_map/ppermute | solution.py:26
  22.4 3.6 %all-to-all-done.r_ref.refs_0_ = bf16[8,192,128]{2,1,0:T(8,128)(2,1)S(1)} async-done(((bf16[8,192,128]{2,1,0:T(8,128)(2,1)}), bf16[8,192,128]{2,1,0:T(8,128)(2,1)S(1)}, u32[]{:S(2)}, u32[]{:S(2)}) %all-to-all-start) | async-done | bytes 393248 | tf_op jit(solution)/shard_map/all_to_all | solution.py:261
  28.8 16.0 %collective-permute-start.16 = (bf16[2,152,512]{2,1,0:T(8,128)(2,1)S(1)}, bf16[2,152,512]{2,1,0:T(8,128)(2,1)S(1)}, u32[]{:S(2)}, u32[]{:S(2)}) collective-permute-start(bf16[2,152,512]{2,1,0:T(8,128)(2,1)S(1)} %pad_maximum_fusion.1.refs_8_), channel_id=1, source_target_pairs={{0,112},{16,0},{32,16},{48,32},{64,48},{80,64},{96,80},{112,96},{1... | collective-permute-start | bytes 933896 | tf_op jit(solution)/shard_map/ppermute | solution.py:26
  44.8 4.4 %collective-permute-done.15.refs_9_ = bf16[2,152,512]{2,1,0:T(8,128)(2,1)S(1)} collective-permute-done((bf16[2,152,512]{2,1,0:T(8,128)(2,1)S(1)}, bf16[2,152,512]{2,1,0:T(8,128)(2,1)S(1)}, u32[]{:S(2)}, u32[]{:S(2)}) %collective-permute-start.15) | collective-permute-done | bytes 311328 | tf_op jit(solution)/shard_map/ppermute | solution.py:26
  49.2 2.5 %collective-permute-start.2 = (bf16[4,128,128]{2,1,0:T(8,128)(2,1)S(1)}, bf16[4,128,128]{2,1,0:T(8,128)(2,1)S(1)}, u32[]{:S(2)}, u32[]{:S(2)}) collective-permute-start(bf16[4,128,128]{2,1,0:T(8,128)(2,1)S(1)} %get-tuple-element.19), channel_id=1, source_target_pairs={{0,12},{4,0},{8,4},{12,8},{1,13},{5,1},{9,5},{13,9},{2,14},{6,2},{... | collective-permute-start | bytes 393224 | tf_op jit(solution)/shard_map/ppermute | solution.py:26
  51.7 2.7 %collective-permute-start.5 = (bf16[4,128,128]{2,1,0:T(8,128)(2,1)S(1)}, bf16[4,128,128]{2,1,0:T(8,128)(2,1)S(1)}, u32[]{:S(2)}, u32[]{:S(2)}) collective-permute-start(bf16[4,128,128]{2,1,0:T(8,128)(2,1)S(1)} %collective-permute-done.3.refs_4_), channel_id=1, source_target_pairs={{0,12},{4,0},{8,4},{12,8},{1,13},{5,1},{9,5},{13,9},{2,14},{6,2},{... | collective-permute-start | bytes 393224 | tf_op jit(solution)/shard_map/ppermute | solution.py:26
  54.4 1.6 %attend_first.1 = (f32[1,1024]{1,0:T(1,128)S(1)}, f32[80,1024]{1,0:T(8,128)S(1)}) custom-call(bf16[8,192,128]{2,1,0:T(8,128)(2,1)S(1)} %all-to-all-done.r_ref.refs_0_), custom_call_target="tpu_custom_call" | custom-call | tf_op jit(solution)/shard_map/attend_first/pallas_call | solution.py:118
  56.0 1.6 %attend_next.2 = (f32[1,1024]{1,0:T(1,128)S(1)}, f32[80,1024]{1,0:T(8,128)S(1)}) custom-call(bf16[8,192,128]{2,1,0:T(8,128)(2,1)S(1)} %all-to-all-done.r_ref.refs_0_, f32[1,1024]{1,0:T(1,128)S(1)} %get-tuple-element.10.refs_1_, f32[80,1024]{1,0:T(8,128)S(1)} %get-tuple-element.11.refs_2_, bf16[4,128,128]{2,1,0:T(8,128)(2,1)S(1)} %collective-permute-done.refs_3_, ...), custom_call_target="tpu_custom_call" | custom-call | tf_op jit(solution)/shard_map/attend_next/pallas_call | solution.py:135
  57.6 1.6 %attend_next.3 = (f32[1,1024]{1,0:T(1,128)S(1)}, f32[80,1024]{1,0:T(8,128)S(1)}) custom-call(bf16[8,192,128]{2,1,0:T(8,128)(2,1)S(1)} %all-to-all-done.r_ref.refs_0_, f32[1,1024]{1,0:T(1,128)S(1)} %get-tuple-element.12.refs_1_, f32[80,1024]{1,0:T(8,128)S(1)} %get-tuple-element.13.refs_2_, bf16[4,128,128]{2,1,0:T(8,128)(2,1)S(1)} %collective-permute-done.2.refs_3_, ...), custom_call_target="tpu_custom_call" | custom-call | tf_op jit(solution)/shard_map/attend_next/pallas_call | solution.py:135
  59.2 2.4 %attend_last.1 = bf16[8,2,64,128]{3,2,1,0:T(8,128)(2,1)} custom-call(bf16[8,192,128]{2,1,0:T(8,128)(2,1)S(1)} %all-to-all-done.r_ref.refs_0_, f32[1,1024]{1,0:T(1,128)S(1)} %get-tuple-element.14.refs_1_, f32[80,1024]{1,0:T(8,128)S(1)} %get-tuple-element.15.refs_2_, bf16[4,128,128]{2,1,0:T(8,128)(2,1)S(1)} %collective-permute-done.4.refs_3_, ...), custom_call_target="tpu_custom_call" | custom-call | tf_op jit(solution)/shard_map/attend_last/pallas_call | solution.py:135
  61.6 6.0 %all-to-all-start.1 = ((bf16[16,64,128]{2,1,0:T(8,128)(2,1)}), bf16[16,64,128]{2,1,0:T(8,128)(2,1)S(1)}, u32[]{:S(2)}, u32[]{:S(2)}) async-start(bf16[16,64,128]{2,1,0:T(8,128)(2,1)} %bitcast.3), calls=%async_computation.1 | async-start | bytes 524288 | tf_op jit(solution)/shard_map/all_to_all | solution.py:277
  67.6 2.7 %collective-permute-start.18 = (bf16[2,152,512]{2,1,0:T(8,128)(2,1)S(1)}, bf16[2,152,512]{2,1,0:T(8,128)(2,1)S(1)}, u32[]{:S(2)}, u32[]{:S(2)}) collective-permute-start(bf16[2,152,512]{2,1,0:T(8,128)(2,1)S(1)} %collective-permute-done.16.refs_10_), channel_id=1, source_target_pairs={{0,112},{16,0},{32,16},{48,32},{64,48},{80,64},{96,80},{112,96},{1... | collective-permute-start | bytes 933896 | tf_op jit(solution)/shard_map/ppermute | solution.py:26
  70.3 10.2 %collective-permute-done.18.refs_12_ = bf16[2,152,512]{2,1,0:T(8,128)(2,1)S(1)} collective-permute-done((bf16[2,152,512]{2,1,0:T(8,128)(2,1)S(1)}, bf16[2,152,512]{2,1,0:T(8,128)(2,1)S(1)}, u32[]{:S(2)}, u32[]{:S(2)}) %collective-permute-start.18) | collective-permute-done | bytes 311328 | tf_op jit(solution)/shard_map/ppermute | solution.py:26
  80.5 2.5 %collective-permute-start.20 = (bf16[2,152,512]{2,1,0:T(8,128)(2,1)S(1)}, bf16[2,152,512]{2,1,0:T(8,128)(2,1)S(1)}, u32[]{:S(2)}, u32[]{:S(2)}) collective-permute-start(bf16[2,152,512]{2,1,0:T(8,128)(2,1)S(1)} %collective-permute-done.18.refs_12_), channel_id=1, source_target_pairs={{0,112},{16,0},{32,16},{48,32},{64,48},{80,64},{96,80},{112,96},{1... | collective-permute-start | bytes 933896 | tf_op jit(solution)/shard_map/ppermute | solution.py:26
  83.6 3.9 %collective-permute-start.7 = (bf16[4,2,64,128]{3,2,1,0:T(8,128)(2,1)}, bf16[4,2,64,128]{3,2,1,0:T(8,128)(2,1)S(1)}, u32[]{:S(2)}, u32[]{:S(2)}) collective-permute-start(bf16[4,2,64,128]{3,2,1,0:T(8,128)(2,1)} %bitcast.5), channel_id=1, source_target_pairs={{0,129},{1,130},{2,131},{3,128},{128,1},{129,2},{130,3},{131,0},{4... | collective-permute-start | bytes 393224 | tf_op jit(solution)/shard_map/ppermute | solution.py:281
  91.0 3.0 %collective-permute-start.23 = (bf16[1,1168,128]{2,1,0:T(8,128)(2,1)}, bf16[1,1168,128]{2,1,0:T(8,128)(2,1)S(1)}, u32[]{:S(2)}, u32[]{:S(2)}) collective-permute-start(bf16[1,1168,128]{2,1,0:T(8,128)(2,1)} %bitcast.19), channel_id=1, source_target_pairs={{0,128},{128,0},{1,129},{129,1},{2,130},{130,2},{3,131},{131,3},{4... | collective-permute-start | bytes 897032 | tf_op jit(solution)/shard_map/ppermute | solution.py:258
  93.9 3.0 %collective-permute-start.9 = (bf16[4,2,64,128]{3,2,1,0:T(8,128)(2,1)}, bf16[4,2,64,128]{3,2,1,0:T(8,128)(2,1)}, u32[]{:S(2)}, u32[]{:S(2)}) collective-permute-start(bf16[4,2,64,128]{3,2,1,0:T(8,128)(2,1)} %bitcast.5), channel_id=1, source_target_pairs={{0,131},{1,128},{2,129},{3,130},{128,3},{129,0},{130,1},{131,2},{4... | collective-permute-start | bytes 393224 | tf_op jit(solution)/shard_map/ppermute | solution.py:281
  97.6 2.7 %collective-permute-start.12 = (bf16[4,2,64,128]{3,2,1,0:T(8,128)(2,1)}, bf16[4,2,64,128]{3,2,1,0:T(8,128)(2,1)}, u32[]{:S(2)}, u32[]{:S(2)}) collective-permute-start(bf16[4,2,64,128]{3,2,1,0:T(8,128)(2,1)} %collective-permute-done.10.refs_5_), channel_id=1, source_target_pairs={{0,3},{1,0},{2,1},{3,2},{4,7},{5,4},{6,5},{7,6},{8,11},{9,8},{10,9... | collective-permute-start | bytes 393224 | tf_op jit(solution)/shard_map/ppermute | solution.py:26
  100.3 2.4 %collective-permute-done.11.refs_6_ = bf16[4,2,64,128]{3,2,1,0:T(8,128)(2,1)} collective-permute-done((bf16[4,2,64,128]{3,2,1,0:T(8,128)(2,1)S(1)}, bf16[4,2,64,128]{3,2,1,0:T(8,128)(2,1)}, u32[]{:S(2)}, u32[]{:S(2)}) %collective-permute-start.11) | collective-permute-done | bytes 131104 | tf_op jit(solution)/shard_map/ppermute | solution.py:26
  103.7 2.2 %project.1 = (f32[2,2,152,128]{3,2,1,0:T(8,128)S(1)}, bf16[2,2,152,128]{3,2,1,0:T(8,128)(2,1)S(1)}) custom-call(s32[3]{0:T(128)S(1)} %pad_add_fusion.refs_0_.at_ref, bf16[8,2,64,128]{3,2,1,0:T(8,128)(2,1)S(1)} %collective-permute-done.6.refs_1_, bf16[4,2,64,128]{3,2,1,0:T(8,128)(2,1)S(1)} %collective-permute-done.7.refs_2_, ...), custom_call_target="tpu_custom_call" | custom-call | tf_op jit(solution)/shard_map/project/pallas_call | solution.py:208
  108.2 1.9 %collective-permute-done.22.refs_2_ = bf16[2,2,152,128]{3,2,1,0:T(8,128)(2,1)S(1)} collective-permute-done((bf16[2,2,152,128]{3,2,1,0:T(8,128)(2,1)S(1)}, bf16[2,2,152,128]{3,2,1,0:T(8,128)(2,1)S(1)}, u32[]{:S(2)}, u32[]{:S(2)}) %collective-permute-start.22) | collective-permute-done | bytes 155680 | tf_op jit(solution)/shard_map/ppermute | solution.py:293
  (48 shorter events, 16.3 us)
Async XLA Ops:
  2.6 23.4 %all-to-all-start = ((bf16[8,192,128]{2,1,0:T(8,128)(2,1)}), bf16[8,192,128]{2,1,0:T(8,128)(2,1)S(1)}, u32[]{:S(2)}, u32[]{:S(2)}) async-start(bf16[8,192,128]{2,1,0:T(8,128)(2,1)} %pack.1), calls=%async_computation | async-start | bytes 786432 | tf_op jit(solution)/shard_map/all_to_all | solution.py:261
  13.8 6.8 %collective-permute-start.14 = (bf16[152,512]{1,0:T(8,128)(2,1)S(1)}, bf16[152,512]{1,0:T(8,128)(2,1)S(1)}, u32[]{:S(2)}, u32[]{:S(2)}) collective-permute-start(bf16[152,512]{1,0:T(8,128)(2,1)S(1)} %get-tuple-element.23), channel_id=1, source_target_pairs={{0,8},{4,12},{8,0},{12,4},{1,9},{5,13},{9,1},{13,5},{2,10},{6,14},... | collective-permute-start | bytes 466952 | tf_op jit(solution)/shard_map/ppermute | solution.py:26
  20.7 28.5 %collective-permute-start.15 = (bf16[2,152,512]{2,1,0:T(8,128)(2,1)S(1)}, bf16[2,152,512]{2,1,0:T(8,128)(2,1)S(1)}, u32[]{:S(2)}, u32[]{:S(2)}) collective-permute-start(bf16[2,152,512]{2,1,0:T(8,128)(2,1)S(1)} %pad_maximum_fusion.1.refs_8_), channel_id=1, source_target_pairs={{0,16},{16,32},{32,48},{48,64},{64,80},{80,96},{96,112},{112,0},{1... | collective-permute-start | bytes 933896 | tf_op jit(solution)/shard_map/ppermute | solution.py:26
  26.0 25.6 %collective-permute-start = (bf16[4,128,128]{2,1,0:T(8,128)(2,1)S(1)}, bf16[4,128,128]{2,1,0:T(8,128)(2,1)S(1)}, u32[]{:S(2)}, u32[]{:S(2)}) collective-permute-start(bf16[4,128,128]{2,1,0:T(8,128)(2,1)S(1)} %get-tuple-element.19), channel_id=1, source_target_pairs={{0,4},{4,8},{8,12},{12,0},{1,5},{5,9},{9,13},{13,1},{2,6},{6,10},{... | collective-permute-start | bytes 393224 | tf_op jit(solution)/shard_map/ppermute | solution.py:26
  27.3 24.3 %collective-permute-start.3 = (bf16[4,128,128]{2,1,0:T(8,128)(2,1)S(1)}, bf16[4,128,128]{2,1,0:T(8,128)(2,1)S(1)}, u32[]{:S(2)}, u32[]{:S(2)}) collective-permute-start(bf16[4,128,128]{2,1,0:T(8,128)(2,1)S(1)} %get-tuple-element.18), channel_id=1, source_target_pairs={{0,12},{4,0},{8,4},{12,8},{1,13},{5,1},{9,5},{13,9},{2,14},{6,2},{... | collective-permute-start | bytes 393224 | tf_op jit(solution)/shard_map/ppermute | solution.py:26
  28.8 25.6 %collective-permute-start.1 = (bf16[4,128,128]{2,1,0:T(8,128)(2,1)S(1)}, bf16[4,128,128]{2,1,0:T(8,128)(2,1)S(1)}, u32[]{:S(2)}, u32[]{:S(2)}) collective-permute-start(bf16[4,128,128]{2,1,0:T(8,128)(2,1)S(1)} %get-tuple-element.18), channel_id=1, source_target_pairs={{0,4},{4,8},{8,12},{12,0},{1,5},{5,9},{9,13},{13,1},{2,6},{6,10},{... | collective-permute-start | bytes 393224 | tf_op jit(solution)/shard_map/ppermute | solution.py:26
  28.8 38.8 %collective-permute-start.16 = (bf16[2,152,512]{2,1,0:T(8,128)(2,1)S(1)}, bf16[2,152,512]{2,1,0:T(8,128)(2,1)S(1)}, u32[]{:S(2)}, u32[]{:S(2)}) collective-permute-start(bf16[2,152,512]{2,1,0:T(8,128)(2,1)S(1)} %pad_maximum_fusion.1.refs_8_), channel_id=1, source_target_pairs={{0,112},{16,0},{32,16},{48,32},{64,48},{80,64},{96,80},{112,96},{1... | collective-permute-start | bytes 933896 | tf_op jit(solution)/shard_map/ppermute | solution.py:26
  49.2 8.4 %collective-permute-start.2 = (bf16[4,128,128]{2,1,0:T(8,128)(2,1)S(1)}, bf16[4,128,128]{2,1,0:T(8,128)(2,1)S(1)}, u32[]{:S(2)}, u32[]{:S(2)}) collective-permute-start(bf16[4,128,128]{2,1,0:T(8,128)(2,1)S(1)} %get-tuple-element.19), channel_id=1, source_target_pairs={{0,12},{4,0},{8,4},{12,8},{1,13},{5,1},{9,5},{13,9},{2,14},{6,2},{... | collective-permute-start | bytes 393224 | tf_op jit(solution)/shard_map/ppermute | solution.py:26
  51.7 7.6 %collective-permute-start.4 = (bf16[4,128,128]{2,1,0:T(8,128)(2,1)S(1)}, bf16[4,128,128]{2,1,0:T(8,128)(2,1)S(1)}, u32[]{:S(2)}, u32[]{:S(2)}) collective-permute-start(bf16[4,128,128]{2,1,0:T(8,128)(2,1)S(1)} %collective-permute-done.refs_3_), channel_id=1, source_target_pairs={{0,4},{4,8},{8,12},{12,0},{1,5},{5,9},{9,13},{13,1},{2,6},{6,10},{... | collective-permute-start | bytes 393224 | tf_op jit(solution)/shard_map/ppermute | solution.py:26
  51.7 7.6 %collective-permute-start.5 = (bf16[4,128,128]{2,1,0:T(8,128)(2,1)S(1)}, bf16[4,128,128]{2,1,0:T(8,128)(2,1)S(1)}, u32[]{:S(2)}, u32[]{:S(2)}) collective-permute-start(bf16[4,128,128]{2,1,0:T(8,128)(2,1)S(1)} %collective-permute-done.3.refs_4_), channel_id=1, source_target_pairs={{0,12},{4,0},{8,4},{12,8},{1,13},{5,1},{9,5},{13,9},{2,14},{6,2},{... | collective-permute-start | bytes 393224 | tf_op jit(solution)/shard_map/ppermute | solution.py:26
  54.4 15.9 %collective-permute-start.17 = (bf16[2,152,512]{2,1,0:T(8,128)(2,1)S(1)}, bf16[2,152,512]{2,1,0:T(8,128)(2,1)S(1)}, u32[]{:S(2)}, u32[]{:S(2)}) collective-permute-start(bf16[2,152,512]{2,1,0:T(8,128)(2,1)S(1)} %collective-permute-done.15.refs_9_), channel_id=1, source_target_pairs={{0,16},{16,32},{32,48},{48,64},{64,80},{80,96},{96,112},{112,0},{1... | collective-permute-start | bytes 933896 | tf_op jit(solution)/shard_map/ppermute | solution.py:26
  61.6 21.3 %all-to-all-start.1 = ((bf16[16,64,128]{2,1,0:T(8,128)(2,1)}), bf16[16,64,128]{2,1,0:T(8,128)(2,1)S(1)}, u32[]{:S(2)}, u32[]{:S(2)}) async-start(bf16[16,64,128]{2,1,0:T(8,128)(2,1)} %bitcast.3), calls=%async_computation.1 | async-start | bytes 524288 | tf_op jit(solution)/shard_map/all_to_all | solution.py:277
  67.6 12.8 %collective-permute-start.18 = (bf16[2,152,512]{2,1,0:T(8,128)(2,1)S(1)}, bf16[2,152,512]{2,1,0:T(8,128)(2,1)S(1)}, u32[]{:S(2)}, u32[]{:S(2)}) collective-permute-start(bf16[2,152,512]{2,1,0:T(8,128)(2,1)S(1)} %collective-permute-done.16.refs_10_), channel_id=1, source_target_pairs={{0,112},{16,0},{32,16},{48,32},{64,48},{80,64},{96,80},{112,96},{1... | collective-permute-start | bytes 933896 | tf_op jit(solution)/shard_map/ppermute | solution.py:26
  70.3 12.7 %collective-permute-start.19 = (bf16[2,152,512]{2,1,0:T(8,128)(2,1)S(1)}, bf16[2,152,512]{2,1,0:T(8,128)(2,1)S(1)}, u32[]{:S(2)}, u32[]{:S(2)}) collective-permute-start(bf16[2,152,512]{2,1,0:T(8,128)(2,1)S(1)} %collective-permute-done.17.refs_11_), channel_id=1, source_target_pairs={{0,16},{16,32},{32,48},{48,64},{64,80},{80,96},{96,112},{112,0},{1... | collective-permute-start | bytes 933896 | tf_op jit(solution)/shard_map/ppermute | solution.py:26
  80.5 8.8 %collective-permute-start.20 = (bf16[2,152,512]{2,1,0:T(8,128)(2,1)S(1)}, bf16[2,152,512]{2,1,0:T(8,128)(2,1)S(1)}, u32[]{:S(2)}, u32[]{:S(2)}) collective-permute-start(bf16[2,152,512]{2,1,0:T(8,128)(2,1)S(1)} %collective-permute-done.18.refs_12_), channel_id=1, source_target_pairs={{0,112},{16,0},{32,16},{48,32},{64,48},{80,64},{96,80},{112,96},{1... | collective-permute-start | bytes 933896 | tf_op jit(solution)/shard_map/ppermute | solution.py:26
  82.9 8.0 %collective-permute-start.21 = (bf16[2,152,512]{2,1,0:T(8,128)(2,1)S(1)}, bf16[2,152,512]{2,1,0:T(8,128)(2,1)S(1)}, u32[]{:S(2)}, u32[]{:S(2)}) collective-permute-start(bf16[2,152,512]{2,1,0:T(8,128)(2,1)S(1)} %collective-permute-done.19.refs_13_), channel_id=1, source_target_pairs={{0,16},{16,32},{32,48},{48,64},{64,80},{80,96},{96,112},{112,0},{1... | collective-permute-start | bytes 933896 | tf_op jit(solution)/shard_map/ppermute | solution.py:26
  83.6 10.3 %collective-permute-start.7 = (bf16[4,2,64,128]{3,2,1,0:T(8,128)(2,1)}, bf16[4,2,64,128]{3,2,1,0:T(8,128)(2,1)S(1)}, u32[]{:S(2)}, u32[]{:S(2)}) collective-permute-start(bf16[4,2,64,128]{3,2,1,0:T(8,128)(2,1)} %bitcast.5), channel_id=1, source_target_pairs={{0,129},{1,130},{2,131},{3,128},{128,1},{129,2},{130,3},{131,0},{4... | collective-permute-start | bytes 393224 | tf_op jit(solution)/shard_map/ppermute | solution.py:281
  87.5 9.4 %collective-permute-start.10 = (bf16[4,2,64,128]{3,2,1,0:T(8,128)(2,1)S(1)}, bf16[4,2,64,128]{3,2,1,0:T(8,128)(2,1)}, u32[]{:S(2)}, u32[]{:S(2)}) collective-permute-start(bf16[4,2,64,128]{3,2,1,0:T(8,128)(2,1)S(1)} %bitcast.17), channel_id=1, source_target_pairs={{0,131},{1,128},{2,129},{3,130},{128,3},{129,0},{130,1},{131,2},{4... | collective-permute-start | bytes 393224 | tf_op jit(solution)/shard_map/ppermute | solution.py:281
  88.7 8.2 %collective-permute-start.8 = (bf16[4,2,64,128]{3,2,1,0:T(8,128)(2,1)S(1)}, bf16[4,2,64,128]{3,2,1,0:T(8,128)(2,1)S(1)}, u32[]{:S(2)}, u32[]{:S(2)}) collective-permute-start(bf16[4,2,64,128]{3,2,1,0:T(8,128)(2,1)S(1)} %bitcast.18), channel_id=1, source_target_pairs={{0,129},{1,130},{2,131},{3,128},{128,1},{129,2},{130,3},{131,0},{4... | collective-permute-start | bytes 393224 | tf_op jit(solution)/shard_map/ppermute | solution.py:281
  89.3 13.5 %collective-permute-start.6 = (bf16[8,2,64,128]{3,2,1,0:T(8,128)(2,1)S(1)}, bf16[8,2,64,128]{3,2,1,0:T(8,128)(2,1)S(1)}, u32[]{:S(2)}, u32[]{:S(2)}) collective-permute-start(bf16[8,2,64,128]{3,2,1,0:T(8,128)(2,1)S(1)} %bitcast.13), channel_id=1, source_target_pairs={{0,128},{1,129},{2,130},{3,131},{128,0},{129,1},{130,2},{131,3},{4... | collective-permute-start | bytes 786440 | tf_op jit(solution)/shard_map/ppermute | solution.py:281
  91.0 17.2 %collective-permute-start.23 = (bf16[1,1168,128]{2,1,0:T(8,128)(2,1)}, bf16[1,1168,128]{2,1,0:T(8,128)(2,1)S(1)}, u32[]{:S(2)}, u32[]{:S(2)}) collective-permute-start(bf16[1,1168,128]{2,1,0:T(8,128)(2,1)} %bitcast.19), channel_id=1, source_target_pairs={{0,128},{128,0},{1,129},{129,1},{2,130},{130,2},{3,131},{131,3},{4... | collective-permute-start | bytes 897032 | tf_op jit(solution)/shard_map/ppermute | solution.py:258
  93.9 6.4 %collective-permute-start.9 = (bf16[4,2,64,128]{3,2,1,0:T(8,128)(2,1)}, bf16[4,2,64,128]{3,2,1,0:T(8,128)(2,1)}, u32[]{:S(2)}, u32[]{:S(2)}) collective-permute-start(bf16[4,2,64,128]{3,2,1,0:T(8,128)(2,1)} %bitcast.5), channel_id=1, source_target_pairs={{0,131},{1,128},{2,129},{3,130},{128,3},{129,0},{130,1},{131,2},{4... | collective-permute-start | bytes 393224 | tf_op jit(solution)/shard_map/ppermute | solution.py:281
  96.9 5.9 %collective-permute-start.11 = (bf16[4,2,64,128]{3,2,1,0:T(8,128)(2,1)S(1)}, bf16[4,2,64,128]{3,2,1,0:T(8,128)(2,1)}, u32[]{:S(2)}, u32[]{:S(2)}) collective-permute-start(bf16[4,2,64,128]{3,2,1,0:T(8,128)(2,1)S(1)} %collective-permute-done.7.refs_2_), channel_id=1, source_target_pairs={{0,1},{1,2},{2,3},{3,0},{4,5},{5,6},{6,7},{7,4},{8,9},{9,10},{10,1... | collective-permute-start | bytes 393224 | tf_op jit(solution)/shard_map/ppermute | solution.py:26
  97.6 5.2 %collective-permute-start.12 = (bf16[4,2,64,128]{3,2,1,0:T(8,128)(2,1)}, bf16[4,2,64,128]{3,2,1,0:T(8,128)(2,1)}, u32[]{:S(2)}, u32[]{:S(2)}) collective-permute-start(bf16[4,2,64,128]{3,2,1,0:T(8,128)(2,1)} %collective-permute-done.10.refs_5_), channel_id=1, source_target_pairs={{0,3},{1,0},{2,1},{3,2},{4,7},{5,4},{6,5},{7,6},{8,11},{9,8},{10,9... | collective-permute-start | bytes 393224 | tf_op jit(solution)/shard_map/ppermute | solution.py:26
  (5 other events, 16.9 us)

commit v3 on v2

--- a/solution.py
+++ b/solution.py
@@ -172,19 +172,18 @@
     return pieces
 
 
-def project_kernel(behind, at_ref, *refs):
+def project_kernel(other, behind, at_ref, *refs):
     c0, c1a, c1b, c3a, c3b, c2a, c2b = refs[:7]
-    ws = refs[7:-4]
-    mine_ref, other_ref, ctx_ref, acc_ref = refs[-4:]
+    ws = refs[7:-3]
+    o_ref, ctx_ref, acc_ref = refs[-3:]
     z, x, y = at_ref[0], at_ref[1], at_ref[2]
-    _, _, dim, rows = c0.shape
+    twin = 1 - x % 2 if other else x % 2
     for d, parts in ((0, (c0,)), (1, (c1a, c1b)), (3, (c3a, c3b)), (2, (c2a, c2b))):
         group = (y + NY - d) % NY
         first = 0
         for part in parts:
-            size = part.shape[0] * dim
-            for twin in range(2):
-                ctx_ref[group, first:first + size, twin * rows:(twin + 1) * rows] = part[:, twin].reshape(size, rows)
+            size = part.shape[0] * part.shape[2]
+            ctx_ref[group, first:first + size, :] = part[:, twin].reshape(size, part.shape[3])
             first += size
     acc_ref[...] = jnp.zeros(acc_ref.shape, F32)
     strip = acc_ref.shape[2]
@@ -193,32 +192,21 @@
         part = jnp.dot(w_ref[...].reshape(2 * strip, w_ref.shape[2]), ctx_ref[zs // 2], preferred_element_type=F32)
         acc_ref[zs % 2, x // 2] += part[:strip]
         acc_ref[zs % 2, 1 - x // 2] += part[strip:]
-    for half in range(2):
-        for i in range(2):
-            left, right = acc_ref[half, i, :, :rows], acc_ref[half, i, :, rows:]
-            second = x % 2 == 1
-            mine_ref[half, i] = jnp.where(second, right, left)
-            other_ref[half, i] = jnp.where(second, left, right).astype(BF16)
-
-
-def project(at, contexts, pieces):
+    o_ref[...] = acc_ref[...].astype(o_ref.dtype)
+
+
+def project(at, contexts, pieces, other):
     behind = [dz for _, dz in pieces]
     rows = contexts[0].shape[3]
     strip = pieces[0][0].shape[1]
     return pl.pallas_call(
-        lambda *refs: project_kernel(behind, *refs),
-        out_shape=(
-            jax.ShapeDtypeStruct((2, 2, strip, rows), F32),
-            jax.ShapeDtypeStruct((2, 2, strip, rows), BF16),
-        ),
+        lambda *refs: project_kernel(other, behind, *refs),
+        out_shape=jax.ShapeDtypeStruct((2, 2, strip, rows), BF16 if other else F32),
         in_specs=[pl.BlockSpec(memory_space=pltpu.SMEM)] + vmem_specs(len(contexts) + len(pieces)),
-        out_specs=tuple(vmem_specs(2)),
-        scratch_shapes=[
-            pltpu.VMEM((NY, 8 * HEAD_DIM, 2 * rows), BF16),
-            pltpu.VMEM((2, 2, strip, 2 * rows), F32),
-        ],
+        out_specs=pl.BlockSpec(memory_space=pltpu.VMEM),
+        scratch_shapes=[pltpu.VMEM((NY, 8 * HEAD_DIM, rows), BF16), pltpu.VMEM((2, 2, strip, rows), F32)],
         compiler_params=pltpu.CompilerParams(vmem_limit_bytes=16 * MIB),
-        name="project",
+        name="project_other" if other else "project_mine",
     )(at, *contexts, *[p[0] for p in pieces])
 
 
@@ -289,7 +277,9 @@
     ctx2a = shift(ctx1a, "mp", NY, 1)
     ctx2b = shift(ctx3b, "mp", NY, -1)
     context = unpack(at, own)
-    mine, other = project(at, (ctx0, ctx1a, ctx1b, ctx3a, ctx3b, ctx2a, ctx2b), pieces)
+    contexts = (ctx0, ctx1a, ctx1b, ctx3a, ctx3b, ctx2a, ctx2b)
+    other = project(at, contexts, pieces, True)
+    mine = project(at, contexts, pieces, False)
     other = lax.ppermute(other, "xl", [(0, 1), (1, 0)])
     handed_t = add_up(at, mine, other, hidden_t, strip)
     return jnp.swapaxes(handed_t, 1, 2), context

time: 114 us -> 112 us (0.982); the launches traced: 111 us -> 111 us
  Pallas kernels: 13 us -> 14.9 us
  local copies, waits for them, and re-layouts: 2.27 us -> 0.72 us
  waiting for transfers between devices: 28 us -> 26.8 us
    ppermute x1, waiting for transfers between devices: 1.86 us -> 0.01 us  [layer(): other = lax.ppermute(other, 'xl', [(0, 1), (1, 0)])]
    unnamed x6 -> x2, local copies, waits for them, and re-layouts: 1.56 us -> 0.01 us
    pallas_call x1 -> x2, Pallas kernels: 2.21 us -> 3.72 us  [project(): pl.pallas_call(lambda *refs: project_kernel(other, behind, *refs), out_sh...]
  transfers between devices with their start and end apart: 26 -> 26, of which waited for: 8 -> 8; matrix products, arithmetic and copies ran while one was open for 1% -> 1% of each run, Pallas kernels for 10% -> 11%
where the time goes in v3:
time: 112 us; the launch traced here: 111 us
  starting transfers between devices  66.3 us (59%)
  waiting for transfers between devices  26.8 us (24%)
  Pallas kernels  14.9 us (13%)
  other arithmetic  1.18 us (1%)
    ppermute x16, starting transfers between devices, shift(): return lax.ppermute(block, axis, [(i, (i + by) % n) for i in range(n)])  36.3 us
    ppermute x16, waiting for transfers between devices, shift(): return lax.ppermute(block, axis, [(i, (i + by) % n) for i in range(n)])  21.9 us
    ppermute x5, starting transfers between devices, turned(): return lax.ppermute(block, ('section', 'mp'), turn)  9.85 us
    all_to_all x1, starting transfers between devices, layer(): r = lax.all_to_all(packed, 'z', 0, 0, tiled=True)  9.13 us
    all_to_all x1, starting transfers between devices, layer(): lax.all_to_all(sent, ('z', 'xl'), 0, 0, tiled=True).reshape(out[0].shape)  5.98 us
    pallas_call x3, Pallas kernels, attend_next(): pl.pallas_call(lambda *refs: next_kernel(last, len(kvs), *refs), out_shap...  5.59 us
    pallas_call x2, Pallas kernels, project(): pl.pallas_call(lambda *refs: project_kernel(other, behind, *refs), out_sh...  3.72 us
    all_to_all x1, waiting for transfers between devices, layer(): r = lax.all_to_all(packed, 'z', 0, 0, tiled=True)  3.6 us
  transfers between devices with their start and end apart: 26, of which 8 were waited for; matrix products, arithmetic and copies ran while one was open for 1% of the time, Pallas kernels for 11%

profile of v3, /device:TPU:1, one launch (start us, length us, event | category | flops | bytes accessed | tf_op | source)
XLA Modules:
  0.0 110.6 jit_solution(9774730825884888778)
XLA Ops:
  2.6 9.1 %all-to-all-start = ((bf16[8,192,128]{2,1,0:T(8,128)(2,1)}), bf16[8,192,128]{2,1,0:T(8,128)(2,1)S(1)}, u32[]{:S(2)}, u32[]{:S(2)}) async-start(bf16[8,192,128]{2,1,0:T(8,128)(2,1)} %pack.1), calls=%async_computation | async-start | bytes 786432 | tf_op jit(solution)/shard_map/all_to_all | solution.py:249
  13.8 2.8 %collective-permute-start.14 = (bf16[152,512]{1,0:T(8,128)(2,1)S(1)}, bf16[152,512]{1,0:T(8,128)(2,1)S(1)}, u32[]{:S(2)}, u32[]{:S(2)}) collective-permute-start(bf16[152,512]{1,0:T(8,128)(2,1)S(1)} %get-tuple-element.19), channel_id=1, source_target_pairs={{0,8},{4,12},{8,0},{12,4},{1,9},{5,13},{9,1},{13,5},{2,10},{6,14},... | collective-permute-start | bytes 466952 | tf_op jit(solution)/shard_map/ppermute | solution.py:26
  16.7 4.0 %collective-permute-done.14 = bf16[152,512]{1,0:T(8,128)(2,1)S(1)} collective-permute-done((bf16[152,512]{1,0:T(8,128)(2,1)S(1)}, bf16[152,512]{1,0:T(8,128)(2,1)S(1)}, u32[]{:S(2)}, u32[]{:S(2)}) %collective-permute-start.14) | collective-permute-done | bytes 155680 | tf_op jit(solution)/shard_map/ppermute | solution.py:26
  20.7 1.7 %collective-permute-start.15 = (bf16[2,152,512]{2,1,0:T(8,128)(2,1)S(1)}, bf16[2,152,512]{2,1,0:T(8,128)(2,1)S(1)}, u32[]{:S(2)}, u32[]{:S(2)}) collective-permute-start(bf16[2,152,512]{2,1,0:T(8,128)(2,1)S(1)} %pad_maximum_fusion.1.refs_8_), channel_id=1, source_target_pairs={{0,16},{16,32},{32,48},{48,64},{64,80},{80,96},{96,112},{112,0},{1... | collective-permute-start | bytes 933896 | tf_op jit(solution)/shard_map/ppermute | solution.py:26
  22.4 3.6 %all-to-all-done.r_ref.refs_0_ = bf16[8,192,128]{2,1,0:T(8,128)(2,1)S(1)} async-done(((bf16[8,192,128]{2,1,0:T(8,128)(2,1)}), bf16[8,192,128]{2,1,0:T(8,128)(2,1)S(1)}, u32[]{:S(2)}, u32[]{:S(2)}) %all-to-all-start) | async-done | bytes 393248 | tf_op jit(solution)/shard_map/all_to_all | solution.py:249
  28.8 16.0 %collective-permute-start.16 = (bf16[2,152,512]{2,1,0:T(8,128)(2,1)S(1)}, bf16[2,152,512]{2,1,0:T(8,128)(2,1)S(1)}, u32[]{:S(2)}, u32[]{:S(2)}) collective-permute-start(bf16[2,152,512]{2,1,0:T(8,128)(2,1)S(1)} %pad_maximum_fusion.1.refs_8_), channel_id=1, source_target_pairs={{0,112},{16,0},{32,16},{48,32},{64,48},{80,64},{96,80},{112,96},{1... | collective-permute-start | bytes 933896 | tf_op jit(solution)/shard_map/ppermute | solution.py:26
  44.8 4.4 %collective-permute-done.15.refs_9_ = bf16[2,152,512]{2,1,0:T(8,128)(2,1)S(1)} collective-permute-done((bf16[2,152,512]{2,1,0:T(8,128)(2,1)S(1)}, bf16[2,152,512]{2,1,0:T(8,128)(2,1)S(1)}, u32[]{:S(2)}, u32[]{:S(2)}) %collective-permute-start.15) | collective-permute-done | bytes 311328 | tf_op jit(solution)/shard_map/ppermute | solution.py:26
  49.2 2.5 %collective-permute-start.2 = (bf16[4,128,128]{2,1,0:T(8,128)(2,1)S(1)}, bf16[4,128,128]{2,1,0:T(8,128)(2,1)S(1)}, u32[]{:S(2)}, u32[]{:S(2)}) collective-permute-start(bf16[4,128,128]{2,1,0:T(8,128)(2,1)S(1)} %get-tuple-element.15), channel_id=1, source_target_pairs={{0,12},{4,0},{8,4},{12,8},{1,13},{5,1},{9,5},{13,9},{2,14},{6,2},{... | collective-permute-start | bytes 393224 | tf_op jit(solution)/shard_map/ppermute | solution.py:26
  51.7 2.7 %collective-permute-start.5 = (bf16[4,128,128]{2,1,0:T(8,128)(2,1)S(1)}, bf16[4,128,128]{2,1,0:T(8,128)(2,1)S(1)}, u32[]{:S(2)}, u32[]{:S(2)}) collective-permute-start(bf16[4,128,128]{2,1,0:T(8,128)(2,1)S(1)} %collective-permute-done.3.refs_4_), channel_id=1, source_target_pairs={{0,12},{4,0},{8,4},{12,8},{1,13},{5,1},{9,5},{13,9},{2,14},{6,2},{... | collective-permute-start | bytes 393224 | tf_op jit(solution)/shard_map/ppermute | solution.py:26
  56.0 1.6 %attend_next.2 = (f32[1,1024]{1,0:T(1,128)S(1)}, f32[80,1024]{1,0:T(8,128)S(1)}) custom-call(bf16[8,192,128]{2,1,0:T(8,128)(2,1)S(1)} %all-to-all-done.r_ref.refs_0_, f32[1,1024]{1,0:T(1,128)S(1)} %get-tuple-element.8.refs_1_, f32[80,1024]{1,0:T(8,128)S(1)} %get-tuple-element.9.refs_2_, bf16[4,128,128]{2,1,0:T(8,128)(2,1)S(1)} %collective-permute-done.refs_3_, ...), custom_call_target="tpu_custom_call" | custom-call | tf_op jit(solution)/shard_map/attend_next/pallas_call | solution.py:135
  57.6 1.6 %attend_next.3 = (f32[1,1024]{1,0:T(1,128)S(1)}, f32[80,1024]{1,0:T(8,128)S(1)}) custom-call(bf16[8,192,128]{2,1,0:T(8,128)(2,1)S(1)} %all-to-all-done.r_ref.refs_0_, f32[1,1024]{1,0:T(1,128)S(1)} %get-tuple-element.10.refs_1_, f32[80,1024]{1,0:T(8,128)S(1)} %get-tuple-element.11.refs_2_, bf16[4,128,128]{2,1,0:T(8,128)(2,1)S(1)} %collective-permute-done.2.refs_3_, ...), custom_call_target="tpu_custom_call" | custom-call | tf_op jit(solution)/shard_map/attend_next/pallas_call | solution.py:135
  59.2 2.4 %attend_last.1 = bf16[8,2,64,128]{3,2,1,0:T(8,128)(2,1)} custom-call(bf16[8,192,128]{2,1,0:T(8,128)(2,1)S(1)} %all-to-all-done.r_ref.refs_0_, f32[1,1024]{1,0:T(1,128)S(1)} %get-tuple-element.12.refs_1_, f32[80,1024]{1,0:T(8,128)S(1)} %get-tuple-element.13.refs_2_, bf16[4,128,128]{2,1,0:T(8,128)(2,1)S(1)} %collective-permute-done.4.refs_3_, ...), custom_call_target="tpu_custom_call" | custom-call | tf_op jit(solution)/shard_map/attend_last/pallas_call | solution.py:135
  61.6 6.0 %all-to-all-start.1 = ((bf16[16,64,128]{2,1,0:T(8,128)(2,1)}), bf16[16,64,128]{2,1,0:T(8,128)(2,1)S(1)}, u32[]{:S(2)}, u32[]{:S(2)}) async-start(bf16[16,64,128]{2,1,0:T(8,128)(2,1)} %bitcast.3), calls=%async_computation.1 | async-start | bytes 524288 | tf_op jit(solution)/shard_map/all_to_all | solution.py:265
  67.6 2.7 %collective-permute-start.18 = (bf16[2,152,512]{2,1,0:T(8,128)(2,1)S(1)}, bf16[2,152,512]{2,1,0:T(8,128)(2,1)S(1)}, u32[]{:S(2)}, u32[]{:S(2)}) collective-permute-start(bf16[2,152,512]{2,1,0:T(8,128)(2,1)S(1)} %collective-permute-done.16.refs_10_), channel_id=1, source_target_pairs={{0,112},{16,0},{32,16},{48,32},{64,48},{80,64},{96,80},{112,96},{1... | collective-permute-start | bytes 933896 | tf_op jit(solution)/shard_map/ppermute | solution.py:26
  70.3 10.2 %collective-permute-done.18.refs_12_ = bf16[2,152,512]{2,1,0:T(8,128)(2,1)S(1)} collective-permute-done((bf16[2,152,512]{2,1,0:T(8,128)(2,1)S(1)}, bf16[2,152,512]{2,1,0:T(8,128)(2,1)S(1)}, u32[]{:S(2)}, u32[]{:S(2)}) %collective-permute-start.18) | collective-permute-done | bytes 311328 | tf_op jit(solution)/shard_map/ppermute | solution.py:26
  80.4 2.5 %collective-permute-start.20 = (bf16[2,152,512]{2,1,0:T(8,128)(2,1)S(1)}, bf16[2,152,512]{2,1,0:T(8,128)(2,1)S(1)}, u32[]{:S(2)}, u32[]{:S(2)}) collective-permute-start(bf16[2,152,512]{2,1,0:T(8,128)(2,1)S(1)} %collective-permute-done.18.refs_12_), channel_id=1, source_target_pairs={{0,112},{16,0},{32,16},{48,32},{64,48},{80,64},{96,80},{112,96},{1... | collective-permute-start | bytes 933896 | tf_op jit(solution)/shard_map/ppermute | solution.py:26
  83.6 3.9 %collective-permute-start.7 = (bf16[4,2,64,128]{3,2,1,0:T(8,128)(2,1)}, bf16[4,2,64,128]{3,2,1,0:T(8,128)(2,1)S(1)}, u32[]{:S(2)}, u32[]{:S(2)}) collective-permute-start(bf16[4,2,64,128]{3,2,1,0:T(8,128)(2,1)} %bitcast.5), channel_id=1, source_target_pairs={{0,129},{1,130},{2,131},{3,128},{128,1},{129,2},{130,3},{131,0},{4... | collective-permute-start | bytes 393224 | tf_op jit(solution)/shard_map/ppermute | solution.py:269
  91.0 3.0 %collective-permute-start.23 = (bf16[1,1168,128]{2,1,0:T(8,128)(2,1)}, bf16[1,1168,128]{2,1,0:T(8,128)(2,1)}, u32[]{:S(2)}, u32[]{:S(2)}) collective-permute-start(bf16[1,1168,128]{2,1,0:T(8,128)(2,1)} %bitcast.19), channel_id=1, source_target_pairs={{0,128},{128,0},{1,129},{129,1},{2,130},{130,2},{3,131},{131,3},{4... | collective-permute-start | bytes 897032 | tf_op jit(solution)/shard_map/ppermute | solution.py:246
  93.9 3.0 %collective-permute-start.9 = (bf16[4,2,64,128]{3,2,1,0:T(8,128)(2,1)}, bf16[4,2,64,128]{3,2,1,0:T(8,128)(2,1)S(1)}, u32[]{:S(2)}, u32[]{:S(2)}) collective-permute-start(bf16[4,2,64,128]{3,2,1,0:T(8,128)(2,1)} %bitcast.5), channel_id=1, source_target_pairs={{0,131},{1,128},{2,129},{3,130},{128,3},{129,0},{130,1},{131,2},{4... | collective-permute-start | bytes 393224 | tf_op jit(solution)/shard_map/ppermute | solution.py:269
  96.9 2.7 %collective-permute-start.12 = (bf16[4,2,64,128]{3,2,1,0:T(8,128)(2,1)S(1)}, bf16[4,2,64,128]{3,2,1,0:T(8,128)(2,1)}, u32[]{:S(2)}, u32[]{:S(2)}) collective-permute-start(bf16[4,2,64,128]{3,2,1,0:T(8,128)(2,1)S(1)} %collective-permute-done.10.refs_5_), channel_id=1, source_target_pairs={{0,3},{1,0},{2,1},{3,2},{4,7},{5,4},{6,5},{7,6},{8,11},{9,8},{10,9... | collective-permute-start | bytes 393224 | tf_op jit(solution)/shard_map/ppermute | solution.py:26
  99.9 2.8 %collective-permute-done.11.refs_6_ = bf16[4,2,64,128]{3,2,1,0:T(8,128)(2,1)} collective-permute-done((bf16[4,2,64,128]{3,2,1,0:T(8,128)(2,1)S(1)}, bf16[4,2,64,128]{3,2,1,0:T(8,128)(2,1)}, u32[]{:S(2)}, u32[]{:S(2)}) %collective-permute-start.11) | collective-permute-done | bytes 131104 | tf_op jit(solution)/shard_map/ppermute | solution.py:26
  102.8 1.9 %project_other.1 = bf16[2,2,152,128]{3,2,1,0:T(8,128)(2,1)S(1)} custom-call(s32[3]{0:T(128)S(1)} %pad_add_fusion.refs_0_.at_ref, bf16[8,2,64,128]{3,2,1,0:T(8,128)(2,1)S(1)} %collective-permute-done.6.refs_1_, bf16[4,2,64,128]{3,2,1,0:T(8,128)(2,1)S(1)} %collective-permute-done.7.refs_2_, bf16[4,2,64,128]{3,2,1,0:T(8,128)(2,1)S(1)} %collective-permute-done.8.refs_3_, ...), custom_call_target="tpu_custom_call" | custom-call | tf_op jit(solution)/shard_map/project_other/pallas_call | solution.py:202
  106.9 1.9 %project_mine.1.refs_1_ = f32[2,2,152,128]{3,2,1,0:T(8,128)S(1)} custom-call(s32[3]{0:T(128)S(1)} %pad_add_fusion.refs_0_.at_ref, bf16[8,2,64,128]{3,2,1,0:T(8,128)(2,1)S(1)} %collective-permute-done.6.refs_1_, bf16[4,2,64,128]{3,2,1,0:T(8,128)(2,1)S(1)} %collective-permute-done.7.refs_2_, bf16[4,2,64,128]{3,2,1,0:T(8,128)(2,1)S(1)} %collective-permute-done.8.refs_3_, ...), custom_call_target="tpu_custom_call" | custom-call | tf_op jit(solution)/shard_map/project_mine/pallas_call | solution.py:202
  108.8 1.8 %add_up.1 = bf16[1,1168,128]{2,1,0:T(8,128)(2,1)} custom-call(s32[3]{0:T(128)S(1)} %pad_add_fusion.refs_0_.at_ref, f32[2,2,152,128]{3,2,1,0:T(8,128)S(1)} %project_mine.1.refs_1_, bf16[2,2,152,128]{3,2,1,0:T(8,128)(2,1)S(1)} %collective-permute-done.22.refs_2_, bf16[1,1168,128]{2,1,0:T(8,128)(2,1)} %collective-permute-done.23.refs_3_), custom_call_target="tpu_custom_call" | custom-call | tf_op jit(solution)/shard_map/add_up/pallas_call | solution.py:224
  (45 shorter events, 15.3 us)
Async XLA Ops:
  2.6 23.4 %all-to-all-start = ((bf16[8,192,128]{2,1,0:T(8,128)(2,1)}), bf16[8,192,128]{2,1,0:T(8,128)(2,1)S(1)}, u32[]{:S(2)}, u32[]{:S(2)}) async-start(bf16[8,192,128]{2,1,0:T(8,128)(2,1)} %pack.1), calls=%async_computation | async-start | bytes 786432 | tf_op jit(solution)/shard_map/all_to_all | solution.py:249
  13.8 6.8 %collective-permute-start.14 = (bf16[152,512]{1,0:T(8,128)(2,1)S(1)}, bf16[152,512]{1,0:T(8,128)(2,1)S(1)}, u32[]{:S(2)}, u32[]{:S(2)}) collective-permute-start(bf16[152,512]{1,0:T(8,128)(2,1)S(1)} %get-tuple-element.19), channel_id=1, source_target_pairs={{0,8},{4,12},{8,0},{12,4},{1,9},{5,13},{9,1},{13,5},{2,10},{6,14},... | collective-permute-start | bytes 466952 | tf_op jit(solution)/shard_map/ppermute | solution.py:26
  20.7 28.5 %collective-permute-start.15 = (bf16[2,152,512]{2,1,0:T(8,128)(2,1)S(1)}, bf16[2,152,512]{2,1,0:T(8,128)(2,1)S(1)}, u32[]{:S(2)}, u32[]{:S(2)}) collective-permute-start(bf16[2,152,512]{2,1,0:T(8,128)(2,1)S(1)} %pad_maximum_fusion.1.refs_8_), channel_id=1, source_target_pairs={{0,16},{16,32},{32,48},{48,64},{64,80},{80,96},{96,112},{112,0},{1... | collective-permute-start | bytes 933896 | tf_op jit(solution)/shard_map/ppermute | solution.py:26
  26.0 25.6 %collective-permute-start = (bf16[4,128,128]{2,1,0:T(8,128)(2,1)S(1)}, bf16[4,128,128]{2,1,0:T(8,128)(2,1)S(1)}, u32[]{:S(2)}, u32[]{:S(2)}) collective-permute-start(bf16[4,128,128]{2,1,0:T(8,128)(2,1)S(1)} %get-tuple-element.15), channel_id=1, source_target_pairs={{0,4},{4,8},{8,12},{12,0},{1,5},{5,9},{9,13},{13,1},{2,6},{6,10},{... | collective-permute-start | bytes 393224 | tf_op jit(solution)/shard_map/ppermute | solution.py:26
  27.3 24.3 %collective-permute-start.3 = (bf16[4,128,128]{2,1,0:T(8,128)(2,1)S(1)}, bf16[4,128,128]{2,1,0:T(8,128)(2,1)S(1)}, u32[]{:S(2)}, u32[]{:S(2)}) collective-permute-start(bf16[4,128,128]{2,1,0:T(8,128)(2,1)S(1)} %get-tuple-element.14), channel_id=1, source_target_pairs={{0,12},{4,0},{8,4},{12,8},{1,13},{5,1},{9,5},{13,9},{2,14},{6,2},{... | collective-permute-start | bytes 393224 | tf_op jit(solution)/shard_map/ppermute | solution.py:26
  28.8 25.6 %collective-permute-start.1 = (bf16[4,128,128]{2,1,0:T(8,128)(2,1)S(1)}, bf16[4,128,128]{2,1,0:T(8,128)(2,1)S(1)}, u32[]{:S(2)}, u32[]{:S(2)}) collective-permute-start(bf16[4,128,128]{2,1,0:T(8,128)(2,1)S(1)} %get-tuple-element.14), channel_id=1, source_target_pairs={{0,4},{4,8},{8,12},{12,0},{1,5},{5,9},{9,13},{13,1},{2,6},{6,10},{... | collective-permute-start | bytes 393224 | tf_op jit(solution)/shard_map/ppermute | solution.py:26
  28.8 38.8 %collective-permute-start.16 = (bf16[2,152,512]{2,1,0:T(8,128)(2,1)S(1)}, bf16[2,152,512]{2,1,0:T(8,128)(2,1)S(1)}, u32[]{:S(2)}, u32[]{:S(2)}) collective-permute-start(bf16[2,152,512]{2,1,0:T(8,128)(2,1)S(1)} %pad_maximum_fusion.1.refs_8_), channel_id=1, source_target_pairs={{0,112},{16,0},{32,16},{48,32},{64,48},{80,64},{96,80},{112,96},{1... | collective-permute-start | bytes 933896 | tf_op jit(solution)/shard_map/ppermute | solution.py:26
  49.2 8.4 %collective-permute-start.2 = (bf16[4,128,128]{2,1,0:T(8,128)(2,1)S(1)}, bf16[4,128,128]{2,1,0:T(8,128)(2,1)S(1)}, u32[]{:S(2)}, u32[]{:S(2)}) collective-permute-start(bf16[4,128,128]{2,1,0:T(8,128)(2,1)S(1)} %get-tuple-element.15), channel_id=1, source_target_pairs={{0,12},{4,0},{8,4},{12,8},{1,13},{5,1},{9,5},{13,9},{2,14},{6,2},{... | collective-permute-start | bytes 393224 | tf_op jit(solution)/shard_map/ppermute | solution.py:26
  51.7 7.6 %collective-permute-start.4 = (bf16[4,128,128]{2,1,0:T(8,128)(2,1)S(1)}, bf16[4,128,128]{2,1,0:T(8,128)(2,1)S(1)}, u32[]{:S(2)}, u32[]{:S(2)}) collective-permute-start(bf16[4,128,128]{2,1,0:T(8,128)(2,1)S(1)} %collective-permute-done.refs_3_), channel_id=1, source_target_pairs={{0,4},{4,8},{8,12},{12,0},{1,5},{5,9},{9,13},{13,1},{2,6},{6,10},{... | collective-permute-start | bytes 393224 | tf_op jit(solution)/shard_map/ppermute | solution.py:26
  51.7 7.6 %collective-permute-start.5 = (bf16[4,128,128]{2,1,0:T(8,128)(2,1)S(1)}, bf16[4,128,128]{2,1,0:T(8,128)(2,1)S(1)}, u32[]{:S(2)}, u32[]{:S(2)}) collective-permute-start(bf16[4,128,128]{2,1,0:T(8,128)(2,1)S(1)} %collective-permute-done.3.refs_4_), channel_id=1, source_target_pairs={{0,12},{4,0},{8,4},{12,8},{1,13},{5,1},{9,5},{13,9},{2,14},{6,2},{... | collective-permute-start | bytes 393224 | tf_op jit(solution)/shard_map/ppermute | solution.py:26
  54.3 15.9 %collective-permute-start.17 = (bf16[2,152,512]{2,1,0:T(8,128)(2,1)S(1)}, bf16[2,152,512]{2,1,0:T(8,128)(2,1)S(1)}, u32[]{:S(2)}, u32[]{:S(2)}) collective-permute-start(bf16[2,152,512]{2,1,0:T(8,128)(2,1)S(1)} %collective-permute-done.15.refs_9_), channel_id=1, source_target_pairs={{0,16},{16,32},{32,48},{48,64},{64,80},{80,96},{96,112},{112,0},{1... | collective-permute-start | bytes 933896 | tf_op jit(solution)/shard_map/ppermute | solution.py:26
  61.6 21.3 %all-to-all-start.1 = ((bf16[16,64,128]{2,1,0:T(8,128)(2,1)}), bf16[16,64,128]{2,1,0:T(8,128)(2,1)S(1)}, u32[]{:S(2)}, u32[]{:S(2)}) async-start(bf16[16,64,128]{2,1,0:T(8,128)(2,1)} %bitcast.3), calls=%async_computation.1 | async-start | bytes 524288 | tf_op jit(solution)/shard_map/all_to_all | solution.py:265
  67.6 12.8 %collective-permute-start.18 = (bf16[2,152,512]{2,1,0:T(8,128)(2,1)S(1)}, bf16[2,152,512]{2,1,0:T(8,128)(2,1)S(1)}, u32[]{:S(2)}, u32[]{:S(2)}) collective-permute-start(bf16[2,152,512]{2,1,0:T(8,128)(2,1)S(1)} %collective-permute-done.16.refs_10_), channel_id=1, source_target_pairs={{0,112},{16,0},{32,16},{48,32},{64,48},{80,64},{96,80},{112,96},{1... | collective-permute-start | bytes 933896 | tf_op jit(solution)/shard_map/ppermute | solution.py:26
  70.3 12.7 %collective-permute-start.19 = (bf16[2,152,512]{2,1,0:T(8,128)(2,1)S(1)}, bf16[2,152,512]{2,1,0:T(8,128)(2,1)S(1)}, u32[]{:S(2)}, u32[]{:S(2)}) collective-permute-start(bf16[2,152,512]{2,1,0:T(8,128)(2,1)S(1)} %collective-permute-done.17.refs_11_), channel_id=1, source_target_pairs={{0,16},{16,32},{32,48},{48,64},{64,80},{80,96},{96,112},{112,0},{1... | collective-permute-start | bytes 933896 | tf_op jit(solution)/shard_map/ppermute | solution.py:26
  80.4 8.8 %collective-permute-start.20 = (bf16[2,152,512]{2,1,0:T(8,128)(2,1)S(1)}, bf16[2,152,512]{2,1,0:T(8,128)(2,1)S(1)}, u32[]{:S(2)}, u32[]{:S(2)}) collective-permute-start(bf16[2,152,512]{2,1,0:T(8,128)(2,1)S(1)} %collective-permute-done.18.refs_12_), channel_id=1, source_target_pairs={{0,112},{16,0},{32,16},{48,32},{64,48},{80,64},{96,80},{112,96},{1... | collective-permute-start | bytes 933896 | tf_op jit(solution)/shard_map/ppermute | solution.py:26
  82.9 8.0 %collective-permute-start.21 = (bf16[2,152,512]{2,1,0:T(8,128)(2,1)S(1)}, bf16[2,152,512]{2,1,0:T(8,128)(2,1)S(1)}, u32[]{:S(2)}, u32[]{:S(2)}) collective-permute-start(bf16[2,152,512]{2,1,0:T(8,128)(2,1)S(1)} %collective-permute-done.19.refs_13_), channel_id=1, source_target_pairs={{0,16},{16,32},{32,48},{48,64},{64,80},{80,96},{96,112},{112,0},{1... | collective-permute-start | bytes 933896 | tf_op jit(solution)/shard_map/ppermute | solution.py:26
  83.6 10.3 %collective-permute-start.7 = (bf16[4,2,64,128]{3,2,1,0:T(8,128)(2,1)}, bf16[4,2,64,128]{3,2,1,0:T(8,128)(2,1)S(1)}, u32[]{:S(2)}, u32[]{:S(2)}) collective-permute-start(bf16[4,2,64,128]{3,2,1,0:T(8,128)(2,1)} %bitcast.5), channel_id=1, source_target_pairs={{0,129},{1,130},{2,131},{3,128},{128,1},{129,2},{130,3},{131,0},{4... | collective-permute-start | bytes 393224 | tf_op jit(solution)/shard_map/ppermute | solution.py:269
  87.5 9.4 %collective-permute-start.10 = (bf16[4,2,64,128]{3,2,1,0:T(8,128)(2,1)S(1)}, bf16[4,2,64,128]{3,2,1,0:T(8,128)(2,1)S(1)}, u32[]{:S(2)}, u32[]{:S(2)}) collective-permute-start(bf16[4,2,64,128]{3,2,1,0:T(8,128)(2,1)S(1)} %bitcast.17), channel_id=1, source_target_pairs={{0,131},{1,128},{2,129},{3,130},{128,3},{129,0},{130,1},{131,2},{4... | collective-permute-start | bytes 393224 | tf_op jit(solution)/shard_map/ppermute | solution.py:269
  88.7 8.2 %collective-permute-start.8 = (bf16[4,2,64,128]{3,2,1,0:T(8,128)(2,1)S(1)}, bf16[4,2,64,128]{3,2,1,0:T(8,128)(2,1)S(1)}, u32[]{:S(2)}, u32[]{:S(2)}) collective-permute-start(bf16[4,2,64,128]{3,2,1,0:T(8,128)(2,1)S(1)} %bitcast.18), channel_id=1, source_target_pairs={{0,129},{1,130},{2,131},{3,128},{128,1},{129,2},{130,3},{131,0},{4... | collective-permute-start | bytes 393224 | tf_op jit(solution)/shard_map/ppermute | solution.py:269
  89.3 13.5 %collective-permute-start.6 = (bf16[8,2,64,128]{3,2,1,0:T(8,128)(2,1)S(1)}, bf16[8,2,64,128]{3,2,1,0:T(8,128)(2,1)S(1)}, u32[]{:S(2)}, u32[]{:S(2)}) collective-permute-start(bf16[8,2,64,128]{3,2,1,0:T(8,128)(2,1)S(1)} %bitcast.13), channel_id=1, source_target_pairs={{0,128},{1,129},{2,130},{3,131},{128,0},{129,1},{130,2},{131,3},{4... | collective-permute-start | bytes 786440 | tf_op jit(solution)/shard_map/ppermute | solution.py:269
  91.0 17.9 %collective-permute-start.23 = (bf16[1,1168,128]{2,1,0:T(8,128)(2,1)}, bf16[1,1168,128]{2,1,0:T(8,128)(2,1)}, u32[]{:S(2)}, u32[]{:S(2)}) collective-permute-start(bf16[1,1168,128]{2,1,0:T(8,128)(2,1)} %bitcast.19), channel_id=1, source_target_pairs={{0,128},{128,0},{1,129},{129,1},{2,130},{130,2},{3,131},{131,3},{4... | collective-permute-start | bytes 897032 | tf_op jit(solution)/shard_map/ppermute | solution.py:246
  93.9 6.0 %collective-permute-start.9 = (bf16[4,2,64,128]{3,2,1,0:T(8,128)(2,1)}, bf16[4,2,64,128]{3,2,1,0:T(8,128)(2,1)S(1)}, u32[]{:S(2)}, u32[]{:S(2)}) collective-permute-start(bf16[4,2,64,128]{3,2,1,0:T(8,128)(2,1)} %bitcast.5), channel_id=1, source_target_pairs={{0,131},{1,128},{2,129},{3,130},{128,3},{129,0},{130,1},{131,2},{4... | collective-permute-start | bytes 393224 | tf_op jit(solution)/shard_map/ppermute | solution.py:269
  96.9 5.9 %collective-permute-start.11 = (bf16[4,2,64,128]{3,2,1,0:T(8,128)(2,1)S(1)}, bf16[4,2,64,128]{3,2,1,0:T(8,128)(2,1)}, u32[]{:S(2)}, u32[]{:S(2)}) collective-permute-start(bf16[4,2,64,128]{3,2,1,0:T(8,128)(2,1)S(1)} %collective-permute-done.7.refs_2_), channel_id=1, source_target_pairs={{0,1},{1,2},{2,3},{3,0},{4,5},{5,6},{6,7},{7,4},{8,9},{9,10},{10,1... | collective-permute-start | bytes 393224 | tf_op jit(solution)/shard_map/ppermute | solution.py:26
  96.9 5.9 %collective-permute-start.12 = (bf16[4,2,64,128]{3,2,1,0:T(8,128)(2,1)S(1)}, bf16[4,2,64,128]{3,2,1,0:T(8,128)(2,1)}, u32[]{:S(2)}, u32[]{:S(2)}) collective-permute-start(bf16[4,2,64,128]{3,2,1,0:T(8,128)(2,1)S(1)} %collective-permute-done.10.refs_5_), channel_id=1, source_target_pairs={{0,3},{1,0},{2,1},{3,2},{4,7},{5,4},{6,5},{7,6},{8,11},{9,8},{10,9... | collective-permute-start | bytes 393224 | tf_op jit(solution)/shard_map/ppermute | solution.py:26
  (3 other events, 15.4 us)
